TPU v7x, 128 devices: a whole 4x4x4 slice. The times are simulated.
128 devices in a mesh: group: 8 (over y, core), local: 16 (over z, x).
Axes of the slice: x: 4, y: 4, z: 4, core: 2. Of those that a mesh axis runs over, the one named last changes fastest.
Arguments:
- hidden_states: bfloat16 [16384, 3584], P(('group', 'local')), may hold values from -6 to 6
- affinity: float32 [16384, 8], P(('group', 'local')), may hold values from 0.1 to 1
- group_ids: int32 [16384, 4], P(('group', 'local')), may hold values from 0 to 7, as said below
- expert_ids: int32 [16384, 8], P(('group', 'local')), may hold values from 0 to 127, as said below
- w_gate: bfloat16 [128, 3584, 1024], P(('group', 'local')), may hold values from -0.09375 to 0.09375
- w_up: bfloat16 [128, 3584, 1024], P(('group', 'local')), may hold values from -0.09375 to 0.09375
- w_down: bfloat16 [128, 1024, 3584], P(('group', 'local')), may hold values from -0.1875 to 0.1875
Outputs:
- routed_out: bfloat16 [16384, 3584], P(('group', 'local'))
Inputs may be any that keep to these rules, and one draw needn't show every extreme that they name: `group_ids`: each row names 4 different groups, and every group is named by exactly 64 of the tokens of one device. `expert_ids`: each row names 8 different experts; columns 2 j and 2 j + 1 lie in group group_ids[t, j]. Of the tokens of one device at most 10 name any one expert, and in every group some expert is named by exactly 10 tokens of every device.
All inputs are finite; a program needn't handle non-finite values.
Results may differ from a plain program's by a relative error of at most 0.007.
Values may be sent and summed in bfloat16 or wider, within the bound.
A program may use at most 128 MiB of HBM per device.

v0:
```python
import jax
import jax.numpy as jnp
from jax import lax
from jax.sharding import PartitionSpec as P

TOP_K = 8
TOPG = 4


def expert_apply(received, gate_mat, up_mat, down_mat):
    shape_in = received.shape
    rows_in = received.reshape(-1, shape_in[-1])
    gate_act = jnp.dot(rows_in, gate_mat, preferred_element_type=jnp.float32)
    up_act = jnp.dot(rows_in, up_mat, preferred_element_type=jnp.float32)
    hidden = (jax.nn.silu(gate_act) * up_act).astype(jnp.bfloat16)
    produced = jnp.dot(hidden, down_mat, preferred_element_type=jnp.float32).astype(jnp.bfloat16)
    return produced.reshape(shape_in)


def shards(hidden_states, affinity, group_ids, expert_ids, w_gate, w_up, w_down):
    tok_rows = hidden_states.shape[0]
    model_width = hidden_states.shape[1]
    group_count = lax.axis_size("group")
    local_count = lax.axis_size("local")
    experts_all = group_count * local_count
    most_rows = 5 * tok_rows * TOP_K // (4 * experts_all)
    pair_size = TOP_K // TOPG
    zero_row = jnp.zeros((), jnp.bfloat16)
    gate_weights = (2.5 * affinity / jnp.sum(affinity, axis=1, keepdims=True)).astype(jnp.bfloat16)
    chosen = jnp.repeat(group_ids, pair_size, axis=1)
    is_valid = expert_ids // local_count == chosen
    mixing = jnp.where(is_valid, gate_weights, zero_row)
    target = jnp.where(is_valid, expert_ids, experts_all)
    member = jnp.sum(
        (target[:, :, None] == jnp.arange(experts_all)[None, None, :]).astype(jnp.int32), axis=1
    )
    before = jnp.cumsum(member, axis=0) - member
    is_slot = (member.T[:, None, :] > 0) & (
        before.T[:, None, :] == jnp.arange(most_rows)[None, :, None]
    )
    source = jnp.sum(jnp.where(is_slot, jnp.arange(tok_rows)[None, None, :], 0), axis=2)
    filled = jnp.any(is_slot, axis=2)
    outgoing = jnp.where(filled[:, :, None], hidden_states[source], zero_row)
    results = lax.all_to_all(
        expert_apply(
            lax.all_to_all(outgoing, ("group", "local"), split_axis=0, concat_axis=0, tiled=True),
            w_gate[0],
            w_up[0],
            w_down[0],
        ),
        ("group", "local"),
        split_axis=0,
        concat_axis=0,
        tiled=True,
    )
    safe_ids = jnp.minimum(target, experts_all - 1)
    slot_pos = safe_ids * most_rows + jnp.take_along_axis(before, safe_ids, axis=1)
    picked = results.reshape(-1, model_width)[slot_pos]
    group_part = jnp.einsum(
        "tgk,tgkd->tgd",
        mixing.reshape(tok_rows, TOPG, pair_size),
        picked.reshape(tok_rows, TOPG, pair_size, model_width),
        preferred_element_type=jnp.float32,
    ).astype(jnp.bfloat16)
    group_part = lax.optimization_barrier(group_part)
    return jnp.sum(group_part.astype(jnp.float32), axis=1).astype(jnp.bfloat16)


def solution(mesh):
    placed = (
        P(("group", "local"), None),
        P(("group", "local"), None),
        P(("group", "local"), None),
        P(("group", "local"), None),
        P(("group", "local"), None, None),
        P(("group", "local"), None, None),
        P(("group", "local"), None, None),
    )
    return jax.shard_map(
        shards, mesh=mesh, in_specs=placed, out_specs=P(("group", "local"), None), check_vma=False
    )
```

profile of v0, /device:TPU:28, one launch (start us, length us, event | category | flops | bytes accessed | tf_op | source)
XLA Modules:
  0.0 566.0 jit_solution(17728102210409597940)
XLA Ops:
  0.0 0.8 broadcast_in_dim.51
  0.8 1.3 bitcast_or_fusion
  2.0 0.6 copy-done.3
  2.7 0.2 convert_reduce_fusion
  3.0 0.2 reduce_window_sum.11
  3.3 0.1 copy.29
  3.4 0.2 select_reduce_fusion
  3.6 0.3 fusion.8
  3.9 0.1 copy.32
  4.0 0.1 reshape.55
  4.2 7.8 %gather_fusion = bf16[1280,3584]{1,0:T(8,128)(2,1)} fusion(bf16[128,3584]{1,0:T(8,128)(2,1)S(1)} %copy-done, s32[2048]{0:T(1024)S(1)} %pad_clamp_fusion), kind=kCustom, calls=%fused_computation | custom fusion | bytes 18355200 | tf_op jit(solution)/shard_map/gather | solution.py:43
  12.0 14.2 %reshape.54 = bf16[128,10,3584]{2,1,0:T(8,128)(2,1)} reshape(bf16[1280,3584]{1,0:T(8,128)(2,1)} %gather_fusion) | data formatting | bytes 18350080 | tf_op jit(solution)/shard_map/gather | solution.py:43
  26.2 0.1 copy.31
  26.3 6.1 %broadcast_select_fusion = bf16[128,10,3584]{2,1,0:T(8,128)(2,1)S(1)} fusion(bf16[128,10,3584]{2,1,0:T(8,128)(2,1)} %reshape.54, pred[128,10]{1,0:T(8,128)(4,1)S(1)} %copy.31), kind=kLoop, calls=%fused_computation.4 | loop fusion | flops 4587520 | bytes 18351360 | tf_op jit(solution)/shard_map/jit(_where)/select_n | solution.py:43
  32.4 173.2 %all_to_all.10 = bf16[128,10,3584]{2,1,0:T(8,128)(2,1)} all-to-all(bf16[128,10,3584]{2,1,0:T(8,128)(2,1)S(1)} %broadcast_select_fusion), channel_id=1, replica_groups=mesh['group'=8,'local'=16] {'group','local'}, dimensions={0} | all-to-all | bytes 18350080 | tf_op jit(solution)/shard_map/all_to_all | solution.py:46
  205.6 14.6 %reshape.48 = bf16[1280,3584]{1,0:T(8,128)(2,1)} reshape(bf16[128,10,3584]{2,1,0:T(8,128)(2,1)} %all_to_all.10) | data formatting | bytes 18350080 | tf_op jit(solution)/shard_map/reshape | solution.py:12
  220.2 13.4 %fusion.1 = f32[1280,1024]{1,0:T(8,128)S(1)} fusion(bf16[1280,3584]{1,0:T(8,128)(2,1)} %reshape.48, bf16[1,3584,1024]{2,1,0:T(8,128)(2,1)} %param.12), kind=kOutput, calls=%fused_computation.7 | convolution fusion | flops 9395240960 | bytes 21757952 | tf_op jit(solution)/shard_map/dot_general | solution.py:14
  233.7 12.7 %multiply_convert_fusion = bf16[1280,1024]{1,0:T(8,128)(2,1)S(1)} fusion(f32[1280,1024]{1,0:T(8,128)S(1)} %fusion.1, bf16[1280,3584]{1,0:T(8,128)(2,1)S(1)} %copy-done.2, bf16[1,3584,1024]{2,1,0:T(8,128)(2,1)} %param.11), kind=kOutput, calls=%fused_computation.11 | convolution fusion | flops 9403105280 | bytes 24379392 | tf_op jit(solution)/shard_map/dot_general | solution.py:13
  246.4 14.9 %convolution_convert_fusion = bf16[1280,3584]{1,0:T(8,128)(2,1)} fusion(bf16[1280,1024]{1,0:T(8,128)(2,1)S(1)} %multiply_convert_fusion, bf16[1,1024,3584]{2,1,0:T(8,128)(2,1)} %param.13), kind=kOutput, calls=%fused_computation.3 | convolution fusion | flops 9399828480 | bytes 19136512 | tf_op jit(solution)/shard_map/dot_general | solution.py:16
  261.3 14.2 %reshape.49 = bf16[128,10,3584]{2,1,0:T(8,128)(2,1)} reshape(bf16[1280,3584]{1,0:T(8,128)(2,1)} %convolution_convert_fusion) | data formatting | bytes 18350080 | tf_op jit(solution)/shard_map/reshape | solution.py:17
  275.5 7.5 %all-to-all-start.1 = ((bf16[128,10,3584]{2,1,0:T(8,128)(2,1)}), bf16[128,10,3584]{2,1,0:T(8,128)(2,1)}, u32[]{:S(2)}, u32[]{:S(2)}) async-start(bf16[128,10,3584]{2,1,0:T(8,128)(2,1)} %reshape.49), calls=%async_computation.1 | async-start | bytes 29360128 | tf_op jit(solution)/shard_map/all_to_all | solution.py:44
  283.0 0.1 copy.33
  283.3 6.8 %gather_fusion.2 = s32[1024]{0:T(1024)S(1)} fusion(s32[128,128]{1,0:T(8,128)S(1)} %sub.14, s32[1024]{0:T(1024)S(1)} %reshape.69), kind=kCustom, calls=%fused_computation.2 | custom fusion | bytes 16384 | tf_op jit(solution)/shard_map/jit(take_along_axis)/gather | solution.py:57
  290.2 0.1 copy.35
  290.5 0.2 copy.36
  290.7 206.1 %all-to-all-done.1 = bf16[128,10,3584]{2,1,0:T(8,128)(2,1)} async-done(((bf16[128,10,3584]{2,1,0:T(8,128)(2,1)}), bf16[128,10,3584]{2,1,0:T(8,128)(2,1)}, u32[]{:S(2)}, u32[]{:S(2)}) %all-to-all-start.1) | async-done | bytes 9175072 | tf_op jit(solution)/shard_map/all_to_all | solution.py:44
  496.8 14.6 %reshape.50 = bf16[1280,3584]{1,0:T(8,128)(2,1)} reshape(bf16[128,10,3584]{2,1,0:T(8,128)(2,1)} %all-to-all-done.1) | data formatting | bytes 18350080 | tf_op jit(solution)/shard_map/reshape | solution.py:58
  511.4 18.6 %gather_fusion.1 = bf16[1024,3584]{1,0:T(8,128)(2,1)} fusion(bf16[1280,3584]{1,0:T(8,128)(2,1)} %reshape.50, s32[1024]{0:T(1024)S(1)} %broadcast_clamp_fusion), kind=kCustom, calls=%fused_computation.1 | custom fusion | bytes 14684160 | tf_op jit(solution)/shard_map/gather | solution.py:58
  529.9 14.9 %reshape.52 = bf16[128,4,2,3584]{3,2,1,0:T(2,128)(2,1)} reshape(bf16[1024,3584]{1,0:T(8,128)(2,1)} %gather_fusion.1) | data formatting | bytes 14680064 | tf_op jit(solution)/shard_map/reshape | solution.py:62
  544.8 10.1 %fusion.14 = bf16[128,4,1,3584]{3,2,1,0:T(2,128)(2,1)S(1)} fusion(bf16[128,4,2,1]{2,3,1,0:T(2,128)(2,1)S(1)} %copy.36, bf16[128,4,2,3584]{3,2,1,0:T(2,128)(2,1)} %reshape.52), kind=kOutput, calls=%fused_computation.36 | convolution fusion | flops 7340032 | bytes 11012096 | tf_op jit(solution)/shard_map/tgk,tgkd->tgd/dot_general | solution.py:59
  554.9 3.7 copy.39
  558.6 7.4 %reduce_sum.45 = bf16[128,3584]{1,0:T(8,128)(2,1)} reduce(bf16[128,4,3584]{2,1,0:T(4,128)(2,1)} %bitcast.35, bf16[]{:T(256)} %constant.49.clone.1), dimensions={1}, to_apply=%region_5.6 | reduce | flops 1376256 | bytes 4587522 | tf_op jit(solution)/shard_map/reduce_sum | solution.py:66
  (27 shorter events, 0.6 us)
Async XLA Ops:
  0.0 4.2 copy-start
  2.0 0.6 copy-start.3
  220.2 13.5 %copy-start.2 = (bf16[1280,3584]{1,0:T(8,128)(2,1)S(1)}, bf16[1280,3584]{1,0:T(8,128)(2,1)}, u32[]{:S(2)}) copy-start(bf16[1280,3584]{1,0:T(8,128)(2,1)} %reshape.48) | copy-start | bytes 27525124
  275.5 221.2 %all-to-all-start.1 = ((bf16[128,10,3584]{2,1,0:T(8,128)(2,1)}), bf16[128,10,3584]{2,1,0:T(8,128)(2,1)}, u32[]{:S(2)}, u32[]{:S(2)}) async-start(bf16[128,10,3584]{2,1,0:T(8,128)(2,1)} %reshape.49), calls=%async_computation.1 | async-start | bytes 29360128 | tf_op jit(solution)/shard_map/all_to_all | solution.py:44
  283.2 7.0 %copy-start.4 = (s32[128,8]{0,1:T(8,128)S(1)}, s32[128,8]{0,1:T(8,128)}, u32[]{:S(2)}) copy-start(s32[128,8]{0,1:T(8,128)} %copy-done.3) | copy-start | bytes 12292
  283.2 7.2 %copy-start.5 = (f32[128,8]{0,1:T(8,128)S(1)}, f32[128,8]{0,1:T(8,128)}, u32[]{:S(2)}) copy-start(f32[128,8]{0,1:T(8,128)} %param.8) | copy-start | bytes 12292
  283.2 7.2 %copy-start.6 = (pred[128,8]{0,1:T(8,128)(4,1)S(1)}, pred[128,8]{0,1:T(8,128)(4,1)}, u32[]{:S(2)}) copy-start(pred[128,8]{0,1:T(8,128)(4,1)} %get-tuple-element.7) | copy-start | bytes 3076
  544.8 21.2 %copy-start.1 = (bf16[128,3584]{1,0:T(8,128)(2,1)S(1)}, bf16[128,3584]{1,0:T(8,128)(2,1)}, u32[]{:S(2)}) copy-start(bf16[128,3584]{1,0:T(8,128)(2,1)} %param.7) | copy-start | bytes 2752516
where the time goes:
time: 568 us; the launch traced here: 566 us
  waiting for transfers between devices  206 us (36%)
  blocking collectives  173 us (30%)
  local copies, waits for them, and re-layouts  112 us (20%)
  matrix products  51.2 us (9%)
  other arithmetic  15.7 us (3%)
  starting transfers between devices  7.48 us (1%)
    all_to_all x1, waiting for transfers between devices, shards(): lax.all_to_all(expert_apply(lax.all_to_all(outgoing, ('group', 'local'),...  206 us
    all_to_all x1, blocking collectives, shards(): lax.all_to_all(outgoing, ('group', 'local'), split_axis=0, concat_axis=0,...  173 us
    gather x2, local copies, waits for them, and re-layouts, shards(): outgoing = jnp.where(filled[:, :, None], hidden_states[source], zero_row)  22 us
    gather x1, local copies, waits for them, and re-layouts, shards(): picked = results.reshape(-1, model_width)[slot_pos]  18.6 us
    reshape x1, local copies, waits for them, and re-layouts, shards(): picked.reshape(tok_rows, TOPG, pair_size, model_width)  14.9 us
    dot_general x1, matrix products, expert_apply(): jnp.dot(hidden, down_mat, preferred_element_type=jnp.float32)  14.9 us
    reshape x1, local copies, waits for them, and re-layouts, expert_apply(): rows_in = received.reshape(-1, shape_in[-1])  14.6 us
    reshape x1, local copies, waits for them, and re-layouts, shards(): picked = results.reshape(-1, model_width)[slot_pos]  14.6 us
  transfers between devices with their start and end apart: 1, of which 1 were waited for; matrix products, arithmetic and copies ran while one was open for 1% of the time, Pallas kernels for 0%

commit v1 on v0

v1 whole, which is shorter than its diff:
```python
import functools

import jax
import jax.numpy as jnp
from jax import lax
from jax.experimental import pallas as pl
from jax.experimental.pallas import tpu as pltpu
from jax.sharding import PartitionSpec as P

TOP_K = 8
TOPG = 4
SIDE = 4
MESH = pl.DeviceIdType.MESH
LAG_X = 1
LAG_C = 3
LAG_F = 5


def position():
    g = lax.axis_index("group")
    l = lax.axis_index("local")
    return g, l // SIDE, l % SIDE


def wait_bytes(ref, sem):
    pltpu.make_async_copy(ref, ref, sem).wait()


def group_peer(g, step, groups):
    return lax.rem(g + step, groups)


def ring_peer(p, step):
    return lax.rem(p + step, SIDE)


def entry_barrier(g, z, x, groups):
    bar = pltpu.get_barrier_semaphore()
    for step in range(1, groups):
        pl.semaphore_signal(
            bar, inc=1, device_id=(group_peer(g, step, groups), z * SIDE + x), device_id_type=MESH
        )
    for step in range(1, SIDE):
        pl.semaphore_signal(bar, inc=1, device_id=(g, ring_peer(z, step) * SIDE + x), device_id_type=MESH)
        pl.semaphore_signal(bar, inc=1, device_id=(g, z * SIDE + ring_peer(x, step)), device_id_type=MESH)
    pl.semaphore_wait(bar, groups - 1 + 2 * (SIDE - 1))


def send_groups(src, dst, chunk, g, z, x, groups, ssem, rsem):
    for step in range(1, groups):
        peer = group_peer(g, step, groups)
        pltpu.make_async_remote_copy(
            src_ref=src.at[chunk, peer],
            dst_ref=dst.at[chunk, g],
            send_sem=ssem,
            recv_sem=rsem.at[chunk],
            device_id=(peer, z * SIDE + x),
            device_id_type=MESH,
        ).start()


def send_z(src, dst, chunk, g, z, x, ssem, rsem):
    for step in (2, 1, 3):
        peer = ring_peer(z, step)
        pltpu.make_async_remote_copy(
            src_ref=src.at[chunk, peer],
            dst_ref=dst.at[chunk, z],
            send_sem=ssem,
            recv_sem=rsem.at[chunk],
            device_id=(g, peer * SIDE + x),
            device_id_type=MESH,
        ).start()
    dst[chunk, z] = src[chunk, z]


def send_x(src, dst, chunk, g, z, x, ssem, rsem):
    for step in (2, 1, 3):
        peer = ring_peer(x, step)
        pltpu.make_async_remote_copy(
            src_ref=src.at[chunk, :, peer],
            dst_ref=dst.at[chunk, :, x],
            send_sem=ssem,
            recv_sem=rsem.at[chunk],
            device_id=(g, z * SIDE + peer),
            device_id_type=MESH,
        ).start()
    for row in range(SIDE):
        dst[chunk, row, x] = src[chunk, row, x]


def dispatch_kernel(
    chunks, groups, slots,
    rt_ref, tok_ref, wg_ref, wu_ref,
    hid_ref, mix_ref, back_ref,
    meta_out, meta_in, first_out, first_in, out_buf, relay, rows,
    acc_g, acc_u, wbuf_g, wbuf_u, pick, sel,
    s_meta, r_meta, s_first, r_first, s_z, r_z, s_x, r_x, w_sem,
):
    g, z, x = position()
    tok = tok_ref.shape[0]
    width = tok_ref.shape[1] // chunks
    seats = tok * TOPG // groups
    held = groups * seats
    block = SIDE * slots
    total = SIDE * block

    def weights(c):
        slot = lax.rem(c, 2)
        start = pl.multiple_of(c * width, width)
        return (
            pltpu.make_async_copy(wg_ref.at[pl.ds(start, width)], wbuf_g.at[slot], w_sem.at[0, slot]),
            pltpu.make_async_copy(wu_ref.at[pl.ds(start, width)], wbuf_u.at[slot], w_sem.at[1, slot]),
        )

    for c in range(2):
        for cp in weights(c):
            cp.start()

    rt = rt_ref[...]
    rt_t = jnp.transpose(rt)
    group_at = lax.broadcasted_iota(jnp.int32, (groups, tok), 0).astype(jnp.float32)
    member = jnp.zeros((groups, tok), jnp.float32)
    for j in range(TOPG):
        member = member + (rt_t[2 * TOP_K + j : 2 * TOP_K + j + 1, :] == group_at).astype(jnp.float32)
    earlier = (
        lax.broadcasted_iota(jnp.int32, (tok, tok), 0) < lax.broadcasted_iota(jnp.int32, (tok, tok), 1)
    ).astype(jnp.bfloat16)
    before = jnp.dot(member.astype(jnp.bfloat16), earlier, preferred_element_type=jnp.float32)
    seat = jnp.where(member > 0, before, -1.0)
    seat_at = lax.broadcasted_iota(jnp.int32, (seats, tok), 0).astype(jnp.float32)
    for gg in range(groups):
        sel[gg * seats : (gg + 1) * seats, :] = (
            (seat_at == seat[gg : gg + 1, :]).astype(jnp.float32).astype(jnp.bfloat16)
        )
    meta = jnp.dot(sel[...], rt.astype(jnp.bfloat16), preferred_element_type=jnp.float32).astype(jnp.bfloat16)
    meta_out[0] = meta.reshape(groups, seats, 128)
    meta_in[0, g] = meta_out[0, g]

    entry_barrier(g, z, x, groups)
    send_groups(meta_out, meta_in, 0, g, z, x, groups, s_meta, r_meta)

    def first(c, carry):
        cols = pl.ds(pl.multiple_of(c * width, width), width)
        got = jnp.dot(sel[...], tok_ref[:, cols], preferred_element_type=jnp.float32).astype(jnp.bfloat16)
        first_out[c] = got.reshape(groups, seats, width)
        first_in[c, g] = first_out[c, g]
        send_groups(first_out, first_in, c, g, z, x, groups, s_first, r_first)
        return carry

    lax.fori_loop(0, chunks, first, 0)

    wait_bytes(meta_in.at[0, pl.ds(0, groups - 1)], r_meta.at[0])
    info = jnp.transpose(meta_in[0].reshape(held, 128).astype(jnp.float32))
    mine = g.astype(jnp.float32)
    ids = [jnp.zeros((1, held), jnp.float32) for _ in range(2)]
    mix = [jnp.zeros((1, held), jnp.float32) for _ in range(2)]
    for j in range(TOPG):
        here = info[2 * TOP_K + j : 2 * TOP_K + j + 1, :] == mine
        for k in range(2):
            ids[k] = ids[k] + jnp.where(here, info[2 * j + k : 2 * j + k + 1, :] + 1.0, 0.0)
            mix[k] = mix[k] + jnp.where(here, info[TOP_K + 2 * j + k : TOP_K + 2 * j + k + 1, :], 0.0)
    experts = SIDE * SIDE
    expert_at = lax.broadcasted_iota(jnp.int32, (experts, held), 0).astype(jnp.float32) + 1.0
    named = (ids[0] == expert_at).astype(jnp.float32) + (ids[1] == expert_at).astype(jnp.float32)
    earlier_row = (
        lax.broadcasted_iota(jnp.int32, (held, held), 0) < lax.broadcasted_iota(jnp.int32, (held, held), 1)
    ).astype(jnp.bfloat16)
    ahead = jnp.dot(named.astype(jnp.bfloat16), earlier_row, preferred_element_type=jnp.float32)
    place = []
    for k in range(2):
        rank = jnp.sum(jnp.where(ids[k] == expert_at, ahead, 0.0), axis=0, keepdims=True)
        place.append(jnp.where(ids[k] > 0, (ids[k] - 1.0) * slots + rank, -1.0))
    row_at = lax.broadcasted_iota(jnp.int32, (block, held), 0).astype(jnp.float32)
    for zz in range(SIDE):
        base = row_at + float(zz * block)
        pick[zz * block : (zz + 1) * block, :] = (
            ((base == place[0]).astype(jnp.float32) + (base == place[1]).astype(jnp.float32)).astype(jnp.bfloat16)
        )

    def step(i, carry):
        @pl.when(i < chunks)
        def _():
            wait_bytes(first_in.at[i, pl.ds(0, groups - 1)], r_first.at[i])
            src = first_in[i].reshape(held, width)
            for zz in range(SIDE):
                got = jnp.dot(
                    pick[zz * block : (zz + 1) * block, :], src, preferred_element_type=jnp.float32
                ).astype(jnp.bfloat16)
                out_buf[i, zz] = got.reshape(SIDE, slots, width)
            send_z(out_buf, relay, i, g, z, x, s_z, r_z)

        @pl.when((i >= LAG_X) & (i < chunks + LAG_X))
        def _():
            c = i - LAG_X
            wait_bytes(relay.at[c, pl.ds(0, SIDE - 1)], r_z.at[c])
            send_x(relay, rows, c, g, z, x, s_x, r_x)

        @pl.when(i == LAG_C)
        def _():
            cols = jnp.concatenate(
                [place[0], place[1], mix[0], mix[1], jnp.zeros((124, held), jnp.float32)], axis=0
            )
            cols = jnp.transpose(cols)
            slot_at = lax.broadcasted_iota(jnp.int32, (held, total), 1).astype(jnp.float32)
            mix_ref[...] = (
                jnp.where(slot_at == cols[:, 0:1], cols[:, 2:3], 0.0)
                + jnp.where(slot_at == cols[:, 1:2], cols[:, 3:4], 0.0)
            ).astype(jnp.bfloat16)
            seat_t = jnp.transpose(
                jnp.concatenate([seat, jnp.full((tok - groups, tok), -1.0, jnp.float32)], axis=0)
            )
            lane = lax.broadcasted_iota(jnp.int32, (tok, held), 1)
            lane_at = lane.astype(jnp.float32)
            back = jnp.zeros((tok, held), jnp.float32)
            for gg in range(groups):
                column = seat_t[:, gg : gg + 1]
                want = jnp.where(column >= 0, column + float(gg * seats), -1.0)
                back = back + (lane_at == want).astype(jnp.float32)
            back_ref[...] = back.astype(jnp.bfloat16)

        @pl.when(i >= LAG_C)
        def _():
            c = i - LAG_C
            slot = lax.rem(c, 2)
            wait_bytes(rows.at[c, pl.ds(0, SIDE - 1)], r_x.at[c])
            for cp in weights(c):
                cp.wait()

            def piece(zz, inner):
                at = pl.ds(pl.multiple_of(zz * block, block), block)
                part = rows[c, zz].reshape(block, width)
                got_g = jnp.dot(part, wbuf_g[slot], preferred_element_type=jnp.float32)
                got_u = jnp.dot(part, wbuf_u[slot], preferred_element_type=jnp.float32)

                @pl.when(c == 0)
                def _():
                    acc_g[at, :] = got_g
                    acc_u[at, :] = got_u

                @pl.when(c > 0)
                def _():
                    acc_g[at, :] = acc_g[at, :] + got_g
                    acc_u[at, :] = acc_u[at, :] + got_u

                return inner

            lax.fori_loop(0, SIDE, piece, 0)

            @pl.when(c + 2 < chunks)
            def _():
                for cp in weights(c + 2):
                    cp.start()

        return carry

    lax.fori_loop(0, chunks + LAG_C, step, 0)

    def finish(b, carry):
        at = pl.ds(pl.multiple_of(b * slots, slots), slots)
        v = acc_g[at, :]
        hid_ref[at, :] = (v / (1.0 + jnp.exp(-v)) * acc_u[at, :]).astype(jnp.bfloat16)
        return carry

    lax.fori_loop(0, total // slots, finish, 0)
    wait_bytes(meta_out.at[0, pl.ds(0, groups - 1)], s_meta)
    wait_bytes(first_out.at[:, pl.ds(0, groups - 1)], s_first)
    wait_bytes(out_buf.at[:, pl.ds(0, SIDE - 1)], s_z)
    wait_bytes(relay.at[:, pl.ds(0, SIDE - 1)], s_x)


def return_kernel(
    chunks, groups, slots,
    hid_ref, mix_ref, back_ref, wd_ref,
    out_ref,
    out_buf, relay, rows, part_out, part_in, wbuf,
    s_z, r_z, s_x, r_x, s_last, r_last, w_sem,
):
    g, z, x = position()
    width = out_ref.shape[1] // chunks
    held = mix_ref.shape[0]
    seats = held // groups
    block = SIDE * slots
    total = SIDE * block

    def weights(c):
        slot = lax.rem(c, 2)
        start = pl.multiple_of(c * width, width)
        return pltpu.make_async_copy(wd_ref.at[:, pl.ds(start, width)], wbuf.at[slot], w_sem.at[slot])

    for c in range(2):
        weights(c).start()
    entry_barrier(g, z, x, groups)

    def step(i, carry):
        @pl.when(i < chunks)
        def _():
            weights(i).wait()
            slot = lax.rem(i, 2)

            def piece(zz, inner):
                at = pl.ds(pl.multiple_of(zz * block, block), block)
                got = jnp.dot(hid_ref[at, :], wbuf[slot], preferred_element_type=jnp.float32).astype(jnp.bfloat16)
                out_buf[i, zz] = got.reshape(SIDE, slots, width)
                return inner

            lax.fori_loop(0, SIDE, piece, 0)
            send_z(out_buf, relay, i, g, z, x, s_z, r_z)

            @pl.when(i + 2 < chunks)
            def _():
                weights(i + 2).start()

        @pl.when((i >= LAG_X) & (i < chunks + LAG_X))
        def _():
            c = i - LAG_X
            wait_bytes(relay.at[c, pl.ds(0, SIDE - 1)], r_z.at[c])
            send_x(relay, rows, c, g, z, x, s_x, r_x)

        @pl.when((i >= LAG_C) & (i < chunks + LAG_C))
        def _():
            c = i - LAG_C
            wait_bytes(rows.at[c, pl.ds(0, SIDE - 1)], r_x.at[c])
            got = jnp.dot(
                mix_ref[...], rows[c].reshape(total, width), preferred_element_type=jnp.float32
            ).astype(jnp.bfloat16)
            part_out[c] = got.reshape(groups, seats, width)
            send_groups(part_out, part_in, c, g, z, x, groups, s_last, r_last)
            part_in[c, g] = part_out[c, g]

        @pl.when(i >= LAG_F)
        def _():
            c = i - LAG_F
            wait_bytes(part_in.at[c, pl.ds(0, groups - 1)], r_last.at[c])
            out_ref[:, pl.ds(pl.multiple_of(c * width, width), width)] = jnp.dot(
                back_ref[...], part_in[c].reshape(held, width), preferred_element_type=jnp.float32
            ).astype(jnp.bfloat16)

        return carry

    lax.fori_loop(0, chunks + LAG_F, step, 0)
    wait_bytes(out_buf.at[:, pl.ds(0, SIDE - 1)], s_z)
    wait_bytes(relay.at[:, pl.ds(0, SIDE - 1)], s_x)
    wait_bytes(part_out.at[:, pl.ds(0, groups - 1)], s_last)


def shards(hidden_states, affinity, group_ids, expert_ids, w_gate, w_up, w_down):
    tok, model = hidden_states.shape
    hid = w_gate.shape[2]
    groups = lax.axis_size("group")
    local = lax.axis_size("local")
    most = 5 * tok * TOP_K // (4 * groups * local)
    slots = most * groups
    seats = tok * TOPG // groups
    held = groups * seats
    total = local * slots
    chunks = 14
    width = model // chunks
    pair = TOP_K // TOPG

    weights = (2.5 * affinity / jnp.sum(affinity, axis=1, keepdims=True)).astype(jnp.bfloat16)
    is_valid = expert_ids // local == jnp.repeat(group_ids, pair, axis=1)
    mixing = jnp.where(is_valid, weights, jnp.zeros((), jnp.bfloat16)).astype(jnp.float32)
    inside = jnp.where(is_valid, expert_ids % local, -1).astype(jnp.float32)
    rt = jnp.concatenate(
        [inside, mixing, group_ids.astype(jnp.float32), jnp.zeros((tok, 128 - 2 * TOP_K - TOPG), jnp.float32)],
        axis=1,
    )

    vmem = pl.BlockSpec(memory_space=pltpu.VMEM)
    anywhere = pl.BlockSpec(memory_space=pl.ANY)
    bf16 = jnp.bfloat16
    dma = pltpu.SemaphoreType.DMA
    hidden, mix, back = pl.pallas_call(
        functools.partial(dispatch_kernel, chunks, groups, slots),
        out_shape=(
            jax.ShapeDtypeStruct((total, hid), bf16),
            jax.ShapeDtypeStruct((held, total), bf16),
            jax.ShapeDtypeStruct((tok, held), bf16),
        ),
        in_specs=[vmem, vmem, anywhere, anywhere],
        out_specs=(vmem, vmem, vmem),
        scratch_shapes=[
            pltpu.VMEM((1, groups, seats, 128), bf16),
            pltpu.VMEM((1, groups, seats, 128), bf16),
            pltpu.VMEM((chunks, groups, seats, width), bf16),
            pltpu.VMEM((chunks, groups, seats, width), bf16),
            pltpu.VMEM((chunks, SIDE, SIDE, slots, width), bf16),
            pltpu.VMEM((chunks, SIDE, SIDE, slots, width), bf16),
            pltpu.VMEM((chunks, SIDE, SIDE, slots, width), bf16),
            pltpu.VMEM((total, hid), jnp.float32),
            pltpu.VMEM((total, hid), jnp.float32),
            pltpu.VMEM((2, width, hid), bf16),
            pltpu.VMEM((2, width, hid), bf16),
            pltpu.VMEM((total, held), bf16),
            pltpu.VMEM((held, tok), bf16),
            dma, dma((1,)), dma, dma((chunks,)), dma, dma((chunks,)), dma, dma((chunks,)), dma((2, 2)),
        ],
        compiler_params=pltpu.CompilerParams(
            collective_id=0, has_side_effects=True, vmem_limit_bytes=60 * 2**20
        ),
        name="dispatch",
    )(rt, hidden_states, w_gate[0], w_up[0])

    return pl.pallas_call(
        functools.partial(return_kernel, chunks, groups, slots),
        out_shape=jax.ShapeDtypeStruct((tok, model), bf16),
        in_specs=[vmem, vmem, vmem, anywhere],
        out_specs=vmem,
        scratch_shapes=[
            pltpu.VMEM((chunks, SIDE, SIDE, slots, width), bf16),
            pltpu.VMEM((chunks, SIDE, SIDE, slots, width), bf16),
            pltpu.VMEM((chunks, SIDE, SIDE, slots, width), bf16),
            pltpu.VMEM((chunks, groups, seats, width), bf16),
            pltpu.VMEM((chunks, groups, seats, width), bf16),
            pltpu.VMEM((2, hid, width), bf16),
            dma, dma((chunks,)), dma, dma((chunks,)), dma, dma((chunks,)), dma((2,)),
        ],
        compiler_params=pltpu.CompilerParams(
            collective_id=1, has_side_effects=True, vmem_limit_bytes=60 * 2**20
        ),
        name="giveback",
    )(hidden, mix, back, w_down[0])


def solution(mesh):
    placed = (
        P(("group", "local"), None),
        P(("group", "local"), None),
        P(("group", "local"), None),
        P(("group", "local"), None),
        P(("group", "local"), None, None),
        P(("group", "local"), None, None),
        P(("group", "local"), None, None),
    )
    return jax.shard_map(
        shards, mesh=mesh, in_specs=placed, out_specs=P(("group", "local"), None), check_vma=False
    )
```

time: 568 us -> 264 us (0.46)
  the two profiles are of different devices: /device:TPU:28 before, /device:TPU:1 now
where the time goes in v1:
time: 264 us; the launch traced here: 263 us
  Pallas kernels  256 us (97%)
  local copies, waits for them, and re-layouts  4.05 us (2%)
  other arithmetic  2.9 us (1%)
    pallas_call x1, Pallas kernels, shards(): pl.pallas_call(functools.partial(dispatch_kernel, chunks, groups, slots),...  134 us
    pallas_call x1, Pallas kernels, shards(): pl.pallas_call(functools.partial(return_kernel, chunks, groups, slots), o...  122 us

profile of v1, /device:TPU:1, one launch (start us, length us, event | category | flops | bytes accessed | tf_op | source)
XLA Modules:
  0.0 263.3 jit_solution(16426015889418499599)
XLA Ops:
  0.0 0.7 reduce_sum.9
  0.7 0.1 pad.3.clone
  0.8 0.7 divide_convert_fusion
  1.5 0.7 convert_element_type.15
  2.2 0.7 broadcast_in_dim.13
  2.8 0.1 copy.31
  3.0 0.1 copy.30
  3.1 0.1 copy.32
  3.2 0.8 copy.26
  4.0 0.1 fusion.2
  4.1 0.7 maximum_maximum_fusion.rt_ref
  4.8 134.2 %dispatch.1 = (bf16[1280,1024]{1,0:T(8,128)(2,1)}, bf16[512,1280]{1,0:T(8,128)(2,1)}, bf16[128,512]{1,0:T(8,128)(2,1)}) custom-call(f32[128,128]{1,0:T(8,128)} %maximum_maximum_fusion.rt_ref, bf16[128,3584]{1,0:T(8,128)(2,1)} %tok_ref.1, bf16[3584,1024]{1,0:T(8,128)(2,1)} %bitcast.4, bf16[3584,1024]{1,0:T(8,128)(2,1)} %bitcast.5), custom_call_target="tpu_custom_call" | custom-call | tf_op jit(solution)/shard_map/dispatch/pallas_call | solution.py:373
  139.0 122.1 %giveback.1 = bf16[128,3584]{1,0:T(8,128)(2,1)} custom-call(bf16[1280,1024]{1,0:T(8,128)(2,1)} %get-tuple-element.8.hid_ref, bf16[512,1280]{1,0:T(8,128)(2,1)} %get-tuple-element.9.mix_ref, bf16[128,512]{1,0:T(8,128)(2,1)} %get-tuple-element.10.back_ref, bf16[1024,3584]{1,0:T(8,128)(2,1)} %bitcast.6), custom_call_target="tpu_custom_call" | custom-call | tf_op jit(solution)/shard_map/giveback/pallas_call | solution.py:404
  261.2 2.2 copy.34
  (2 shorter events, 0.0 us)

commit v2 on v0

v2 whole, which is shorter than its diff:
```python
import functools

import jax
import jax.numpy as jnp
from jax import lax
from jax.experimental import pallas as pl
from jax.experimental.pallas import tpu as pltpu
from jax.sharding import PartitionSpec as P

TOP_K = 8
TOPG = 4
SIDE = 4
MOST = 10
CHUNKS = 14
N_G = 5
N_X = 5
N_Z = 4
LANES = 128
MESH = pl.DeviceIdType.MESH
BF16 = jnp.bfloat16
F32 = jnp.float32


def position():
    g = lax.axis_index("group")
    l = lax.axis_index("local")
    return g, l // SIDE, l % SIDE


def wait_bytes(ref, sem):
    pltpu.make_async_copy(ref, ref, sem).wait()


def ring(p, step):
    return lax.rem(p + step, SIDE)


def remote(src, dst, ssem, rsem, g, z, x):
    pltpu.make_async_remote_copy(
        src_ref=src, dst_ref=dst, send_sem=ssem, recv_sem=rsem, device_id=(g, z * SIDE + x), device_id_type=MESH
    ).start()


def iota(shape, axis):
    return lax.broadcasted_iota(jnp.int32, shape, axis).astype(F32)


def one_hot(mask):
    return jnp.where(mask, 1.0, 0.0).astype(BF16)


def dot(a, b):
    return jnp.dot(a, b, preferred_element_type=F32)


def signal_peers(sem, g, z, x, groups):
    for step in range(1, groups):
        pl.semaphore_signal(
            sem, inc=1, device_id=(lax.rem(g + step, groups), z * SIDE + x), device_id_type=MESH
        )
    for step in range(1, SIDE):
        pl.semaphore_signal(sem, inc=1, device_id=(g, ring(z, step) * SIDE + x), device_id_type=MESH)
        pl.semaphore_signal(sem, inc=1, device_id=(g, z * SIDE + ring(x, step)), device_id_type=MESH)


def entry_barrier(g, z, x, groups):
    bar = pltpu.get_barrier_semaphore()
    signal_peers(bar, g, z, x, groups)
    pl.semaphore_wait(bar, groups - 1 + 2 * (SIDE - 1))


def send_groups(src, dst, c, g, z, x, groups, ssem, rsem):
    for step in range(1, groups):
        peer = lax.rem(g + step, groups)
        remote(src.at[c, peer], dst.at[c, g], ssem, rsem, peer, z, x)
    dst[c, g] = src[c, g]


def send_pairs(src, dst, c, g, z, x, groups, ssem, rsem):
    for step in range(1, groups):
        peer = lax.rem(g + step, groups)
        remote(src.at[c, pl.ds(2 * peer, 2)], dst.at[c, pl.ds(2 * g, 2)], ssem, rsem, peer, z, x)
    dst[c, pl.ds(2 * g, 2)] = src[c, pl.ds(2 * g, 2)]


def along_z(src, sc, dst, dc, g, z, x, ssem, rsem):
    for step in (2, 1, 3):
        peer = ring(z, step)
        remote(src.at[sc, peer], dst.at[dc, z], ssem, rsem, g, peer, x)
    dst[dc, z] = src[sc, z]


def along_x(src, sc, dst, dc, g, z, x, ssem, rsem):
    for step in (2, 1, 3):
        peer = ring(x, step)
        remote(src.at[sc, :, peer], dst.at[dc, :, x], ssem, rsem, g, z, peer)
    for row in range(SIDE):
        dst[dc, row, x] = src[sc, row, x]


def rank_table(eids, mixes, experts, span):
    rows, cols = experts.shape
    named = jnp.zeros((rows, cols), F32)
    weight = jnp.zeros((rows, cols), F32)
    for k in range(TOP_K):
        hit = eids[k] == experts
        named = named + jnp.where(hit, 1.0, 0.0)
        weight = weight + jnp.where(hit, mixes[k], 0.0)
    r = iota((cols, cols), 0)
    c = iota((cols, cols), 1)
    earlier = one_hot((r < c) & (jnp.floor(r / span) == jnp.floor(c / span)))
    ahead = dot(named.astype(BF16), earlier)
    return jnp.where(named > 0, ahead, -1.0), weight


def fill_pick(pick, seat, per_expert, blocks, span):
    total, cols = pick.shape
    rows = seat.shape[0]
    part = total // SIDE
    seat16 = seat.astype(BF16)
    column = 16.0 * jnp.floor(iota((part, cols), 1) / span)
    for p in range(SIDE):
        at = iota((part, rows), 0) + float(p * part)
        spread = one_hot(jnp.floor((at + 0.5) / per_expert) == iota((part, rows), 1))
        slot = iota((part, 1), 0) + float(p * part)
        ten = jnp.floor((slot + 0.5) / MOST)
        code = (slot - MOST * ten) + 16.0 * (ten - blocks * jnp.floor((ten + 0.5) / blocks))
        pick[p * part : (p + 1) * part, :] = one_hot(dot(spread, seat16) + column == code)


def fill_mix(mix, seat, weight, per_expert, blocks, span):
    cols, total = mix.shape
    rows = seat.shape[0]
    both = jnp.concatenate([seat, weight, jnp.zeros((LANES - 2 * rows, cols), F32)], axis=0)
    turned = jnp.transpose(both).astype(BF16)
    owner = jnp.floor((iota((LANES, total), 1) + 0.5) / per_expert)
    lane = iota((LANES, total), 0)
    spread_seat = one_hot(owner == lane)
    spread_mix = one_hot(owner + float(rows) == lane)
    slot = iota((1, total), 1)
    ten = jnp.floor((slot + 0.5) / MOST)
    code = (slot - MOST * ten) + 16.0 * (ten - blocks * jnp.floor((ten + 0.5) / blocks))
    part = cols // SIDE
    for p in range(SIDE):
        here = turned[p * part : (p + 1) * part, :]
        row = 16.0 * jnp.floor((iota((part, 1), 0) + float(p * part)) / span)
        mix[p * part : (p + 1) * part, :] = jnp.where(
            dot(here, spread_seat) + row == code, dot(here, spread_mix), 0.0
        ).astype(BF16)


def fill_swap(swap, outer, inner):
    total = swap.shape[0]
    part = total // SIDE
    lane = iota((part, total), 1)
    for p in range(SIDE):
        slot = iota((part, 1), 0) + float(p * part)
        ten = jnp.floor((slot + 0.5) / MOST)
        o = jnp.floor((ten + 0.5) / inner)
        i = ten - o * inner
        swap[p * part : (p + 1) * part, :] = one_hot(lane == (i * outer + o) * MOST + (slot - MOST * ten))


def read_info(info):
    ids = []
    mixes = []
    for k in range(TOP_K):
        inside = info[k : k + 1, :]
        group = info[2 * TOP_K + k // 2 : 2 * TOP_K + k // 2 + 1, :]
        ids.append(jnp.where(inside >= 0, inside + float(SIDE * SIDE) * group, -1.0))
        mixes.append(info[TOP_K + k : TOP_K + k + 1, :])
    return ids, mixes


def dispatch_kernel(
    groups, slots,
    aff_ref, gid_ref, eid_ref, tok_ref, wg_ref, wu_ref,
    hid_ref, mix_g, mix_x, mix_z, back_ref,
    info_out, info_x, info_z, meta_out, meta_in, first_out, first_in, wide_x, wide_z,
    out_g, relay_g, y_out, y_in, rows, acc_g, acc_u, wbuf_g, wbuf_u, pick_g, pick_x, pick_z, swap, sel, stage,
    s_info, r_info, s_meta, r_meta, s_first, r_first, s_wide_x, s_wide_z, r_wide, s_one, r_one,
    s_two, s_y, r_y, s_end, r_rows, w_sem, mix_sem,
):
    g, z, x = position()
    tok = tok_ref.shape[0]
    width = tok_ref.shape[1] // CHUNKS
    seats = tok * TOPG // groups
    held = groups * seats
    block = SIDE * slots
    total = SIDE * block
    local = SIDE * SIDE

    def columns(c):
        return pl.ds(pl.multiple_of(c * width, width), width)

    def weights(c):
        slot = lax.rem(c, 2)
        return (
            pltpu.make_async_copy(wg_ref.at[columns(c)], wbuf_g.at[slot], w_sem.at[0, slot]),
            pltpu.make_async_copy(wu_ref.at[columns(c)], wbuf_u.at[slot], w_sem.at[1, slot]),
        )

    for c in range(2):
        for cp in weights(c):
            cp.start()

    aff = aff_ref[...]
    scaled = (2.5 * aff / jnp.sum(aff, axis=1, keepdims=True)).astype(BF16)
    gid = gid_ref[...].astype(F32)
    eid = eid_ref[...].astype(F32)
    twice = one_hot(jnp.floor(iota((TOPG, TOP_K), 1) / 2.0) == iota((TOPG, TOP_K), 0))
    chosen = dot(gid.astype(BF16), twice)
    owner = jnp.floor(eid / float(local))
    is_valid = owner == chosen
    mixing = jnp.where(is_valid, scaled.astype(F32), 0.0).astype(BF16)
    inside = jnp.where(is_valid, eid - float(local) * owner, -1.0).astype(BF16)
    lane_of = iota((TOP_K, LANES), 1) - iota((TOP_K, LANES), 0)
    lane_of4 = iota((TOPG, LANES), 1) - iota((TOPG, LANES), 0)
    rt = (
        dot(inside, one_hot(lane_of == 0.0))
        + dot(mixing, one_hot(lane_of == float(TOP_K)))
        + dot(gid.astype(BF16), one_hot(lane_of4 == float(2 * TOP_K)))
    )
    info_out[...] = rt.astype(BF16)
    info_x[x] = info_out[...]
    info_z[z] = info_out[...]

    entry_barrier(g, z, x, groups)
    for step in (2, 1, 3):
        peer = ring(x, step)
        remote(info_out, info_x.at[x], s_info.at[0], r_info.at[0], g, z, peer)
        peer = ring(z, step)
        remote(info_out, info_z.at[z], s_info.at[1], r_info.at[1], g, peer, x)

    rt_t = jnp.transpose(rt)
    group_at = iota((groups, tok), 0)
    member = jnp.zeros((groups, tok), F32)
    for j in range(TOPG):
        member = member + jnp.where(rt_t[2 * TOP_K + j : 2 * TOP_K + j + 1, :] == group_at, 1.0, 0.0)
    earlier = one_hot(iota((tok, tok), 0) < iota((tok, tok), 1))
    seat = jnp.where(member > 0, dot(member.astype(BF16), earlier), -1.0)
    seat_at = iota((seats, tok), 0)
    for gg in range(groups):
        sel[gg * seats : (gg + 1) * seats, :] = one_hot(seat_at == seat[gg : gg + 1, :])
    meta_out[0] = dot(sel[...], info_out[...]).astype(BF16).reshape(groups, seats, LANES)
    send_groups(meta_out, meta_in, 0, g, z, x, groups, s_meta, r_meta)

    def first(t, carry):
        got = dot(sel[...], tok_ref[:, columns(3 * t)]).astype(BF16)
        first_out[t] = got.reshape(groups, seats, width)
        send_groups(first_out, first_in, t, g, z, x, groups, s_first, r_first.at[t])
        wide_x[t, x] = tok_ref[:, columns(3 * t + 1)]
        for step in (2, 1, 3):
            remote(wide_x.at[t, x], wide_x.at[t, x], s_wide_x, r_wide.at[t], g, z, ring(x, step))

        @pl.when(t < N_Z)
        def _():
            wide_z[t, z] = tok_ref[:, columns(3 * t + 2)]
            for step in (2, 1, 3):
                remote(wide_z.at[t, z], wide_z.at[t, z], s_wide_z, r_wide.at[N_X + t], g, ring(z, step), x)

        return carry

    lax.fori_loop(0, N_G, first, 0)

    row = iota((2 * local, held), 0)
    wait_bytes(info_x.at[pl.ds(0, SIDE - 1)], r_info.at[0])
    ids, mixes = read_info(jnp.transpose(info_x[...].reshape(held, LANES).astype(F32)))
    seat_x, weight_x = rank_table(ids, mixes, row * float(SIDE) + x.astype(F32), float(tok))
    fill_pick(pick_x, seat_x, float(SIDE * MOST), float(SIDE), float(tok))
    wait_bytes(meta_in.at[0, pl.ds(0, groups - 1)], r_meta)
    ids, mixes = read_info(jnp.transpose(meta_in[0].reshape(held, LANES).astype(F32)))
    seat_g, weight_g = rank_table(
        ids, mixes, iota((local, held), 0) + float(local) * g.astype(F32), float(seats)
    )
    fill_pick(pick_g, seat_g, float(slots), float(groups), float(seats))
    wait_bytes(info_z.at[pl.ds(0, SIDE - 1)], r_info.at[1])
    ids, mixes = read_info(jnp.transpose(info_z[...].reshape(held, LANES).astype(F32)))
    own = jnp.floor(row / float(SIDE)) * float(local - SIDE) + row + float(SIDE) * z.astype(F32)
    seat_z, weight_z = rank_table(ids, mixes, own, float(tok))
    fill_pick(pick_z, seat_z, float(SIDE * MOST), float(SIDE), float(tok))

    def to_peers(c, src, pick):
        for p in range(SIDE):
            got = dot(pick[p * block : (p + 1) * block, :], src).astype(BF16)
            y_out[c, pl.ds(p * SIDE, SIDE)] = got.reshape(SIDE, slots, width)
        send_pairs(y_out, y_in, c, g, z, x, groups, s_y.at[c], r_y.at[c])

    def reorder(c):
        wait_bytes(y_in.at[c, pl.ds(0, 2 * groups - 2)], r_y.at[c])
        wait_bytes(y_out.at[c, pl.ds(0, 2 * groups - 2)], s_y.at[c])
        src = y_in[c].reshape(total, width)
        for p in range(SIDE):
            got = dot(swap[p * block : (p + 1) * block, :], src).astype(BF16)
            y_out[c, pl.ds(p * SIDE, SIDE)] = got.reshape(SIDE, slots, width)

    def step(t, carry):
        @pl.when(t < N_G)
        def _():
            wait_bytes(first_in.at[t, pl.ds(0, groups - 1)], r_first.at[t])
            src = first_in[t].reshape(held, width)
            for p in range(SIDE):
                got = dot(pick_g[p * block : (p + 1) * block, :], src).astype(BF16)
                out_g[t, p] = got.reshape(SIDE, slots, width)

            @pl.when(lax.rem(t, 2) == 0)
            def _():
                along_x(out_g, t, relay_g, t, g, z, x, s_one, r_one.at[t])

            @pl.when(lax.rem(t, 2) == 1)
            def _():
                along_z(out_g, t, relay_g, t, g, z, x, s_one, r_one.at[t])

        @pl.when(t < N_X)
        def _():
            wait_bytes(wide_x.at[t, pl.ds(0, SIDE - 1)], r_wide.at[t])
            to_peers(t, wide_x[t].reshape(held, width), pick_x)

        @pl.when(t < N_Z)
        def _():
            wait_bytes(wide_z.at[t, pl.ds(0, SIDE - 1)], r_wide.at[N_X + t])
            to_peers(N_X + t, wide_z[t].reshape(held, width), pick_z)

        @pl.when(t == 0)
        def _():
            fill_swap(swap, local, groups)

        @pl.when((t >= 1) & (t < N_G + 1))
        def _():
            c = t - 1
            wait_bytes(relay_g.at[c, pl.ds(0, SIDE - 1)], r_one.at[c])

            @pl.when(lax.rem(c, 2) == 0)
            def _():
                along_z(relay_g, c, rows, 3 * c, g, z, x, s_two, r_rows.at[3 * c])

            @pl.when(lax.rem(c, 2) == 1)
            def _():
                along_x(relay_g, c, rows, 3 * c, g, z, x, s_two, r_rows.at[3 * c])

        @pl.when((t >= 1) & (t < N_X + 1))
        def _():
            c = t - 1
            reorder(c)
            for step in (2, 1, 3):
                peer = ring(z, step)
                remote(
                    y_out.at[c, pl.ds(SIDE * peer, SIDE)], rows.at[3 * c + 1, z], s_end, r_rows.at[3 * c + 1],
                    g, peer, x,
                )
            rows[3 * c + 1, z] = y_out[c, pl.ds(SIDE * z, SIDE)]

        @pl.when((t >= 1) & (t < N_Z + 1))
        def _():
            c = t - 1
            reorder(N_X + c)
            for step in (2, 1, 3):
                peer = ring(x, step)
                remote(
                    y_out.at[N_X + c, pl.ds(SIDE * peer, SIDE)], rows.at[3 * c + 2, :, x], s_end,
                    r_rows.at[3 * c + 2], g, z, peer,
                )
            for p in range(SIDE):
                rows[3 * c + 2, p, x] = y_out[N_X + c, SIDE * x + p]

        @pl.when(t == 1)
        def _():
            def keep(mix):
                put = pltpu.make_async_copy(stage, mix, mix_sem)
                put.start()
                put.wait()

            fill_mix(stage, seat_g, weight_g, float(slots), float(groups), float(seats))
            keep(mix_g)
            fill_mix(stage, seat_x, weight_x, float(SIDE * MOST), float(SIDE), float(tok))
            keep(mix_x)
            fill_mix(stage, seat_z, weight_z, float(SIDE * MOST), float(SIDE), float(tok))
            keep(mix_z)
            seat_t = jnp.transpose(jnp.concatenate([seat, jnp.full((tok - groups, tok), -1.0, F32)], axis=0))
            lane_at = iota((tok, held), 1)
            back = jnp.zeros((tok, held), F32)
            for gg in range(groups):
                column = seat_t[:, gg : gg + 1]
                want = jnp.where(column >= 0, column + float(gg * seats), -1.0)
                back = back + jnp.where(lane_at == want, 1.0, 0.0)
            back_ref[...] = back.astype(BF16)

        def multiply(c, carry_in):
            slot = lax.rem(c, 2)
            wait_bytes(rows.at[c, pl.ds(0, SIDE - 1)], r_rows.at[c])
            for cp in weights(c):
                cp.wait()

            def piece(p, inner):
                at = pl.ds(pl.multiple_of(p * block, block), block)
                part = rows[c, p].reshape(block, width)
                got_g = dot(part, wbuf_g[slot])
                got_u = dot(part, wbuf_u[slot])

                @pl.when(c == 0)
                def _():
                    acc_g[at, :] = got_g
                    acc_u[at, :] = got_u

                @pl.when(c > 0)
                def _():
                    acc_g[at, :] = acc_g[at, :] + got_g
                    acc_u[at, :] = acc_u[at, :] + got_u

                return inner

            lax.fori_loop(0, SIDE, piece, 0)

            @pl.when(c + 2 < CHUNKS)
            def _():
                for cp in weights(c + 2):
                    cp.start()

            return carry_in

        @pl.when(t >= 2)
        def _():
            low = 3 * (t - 2)
            lax.fori_loop(low, jnp.minimum(low + 3, CHUNKS), multiply, 0)

        return carry

    lax.fori_loop(0, N_G + 2, step, 0)

    def finish(b, carry):
        at = pl.ds(pl.multiple_of(b * slots, slots), slots)
        v = acc_g[at, :]
        hid_ref[at, :] = (v / (1.0 + jnp.exp(-v)) * acc_u[at, :]).astype(BF16)
        return carry

    lax.fori_loop(0, total // slots, finish, 0)
    wait_bytes(info_x.at[pl.ds(0, SIDE - 1)], s_info.at[0])
    wait_bytes(info_z.at[pl.ds(0, SIDE - 1)], s_info.at[1])
    wait_bytes(meta_out.at[0, pl.ds(0, groups - 1)], s_meta)
    wait_bytes(first_out.at[:, pl.ds(0, groups - 1)], s_first)
    wait_bytes(wide_x.at[:, pl.ds(0, SIDE - 1)], s_wide_x)
    wait_bytes(wide_z.at[:, pl.ds(0, SIDE - 1)], s_wide_z)
    wait_bytes(out_g.at[:, pl.ds(0, SIDE - 1)], s_one)
    wait_bytes(relay_g.at[:, pl.ds(0, SIDE - 1)], s_two)
    wait_bytes(y_out.at[:, pl.ds(0, SIDE * (SIDE - 1))], s_end)


def return_kernel(
    groups, slots,
    hid_ref, mix_g, mix_x, mix_z, back_ref, wd_ref,
    out_ref,
    out_buf, relay_g, rows_g, mid, y_out, y_in, part_out, part_in, sum_out, sum_in, wbuf, swap,
    s_one, r_one, s_two, r_two, s_mid, r_mid, s_y, r_y, s_last, r_last, s_sum_x, s_sum_z, r_sum, w_sem,
):
    g, z, x = position()
    tok = out_ref.shape[0]
    width = out_ref.shape[1] // CHUNKS
    held = mix_g.shape[0]
    seats = held // groups
    block = SIDE * slots
    total = SIDE * block

    def columns(c):
        return pl.ds(pl.multiple_of(c * width, width), width)

    def weights(c):
        slot = lax.rem(c, 2)
        return pltpu.make_async_copy(wd_ref.at[:, columns(c)], wbuf.at[slot], w_sem.at[slot])

    for c in range(2):
        weights(c).start()
    entry_barrier(g, z, x, groups)

    def down(c):
        slot = lax.rem(c, 2)
        weights(c).wait()

        def piece(p, inner):
            at = pl.ds(pl.multiple_of(p * block, block), block)
            got = dot(hid_ref[at, :], wbuf[slot]).astype(BF16)
            out_buf[c, p] = got.reshape(SIDE, slots, width)
            return inner

        lax.fori_loop(0, SIDE, piece, 0)

        @pl.when(c + 2 < CHUNKS)
        def _():
            weights(c + 2).start()

    def to_sources(c):
        wait_bytes(mid.at[c, pl.ds(0, SIDE * (SIDE - 1))], r_mid.at[c])
        src = mid[c].reshape(total, width)
        for p in range(SIDE):
            got = dot(swap[p * block : (p + 1) * block, :], src).astype(BF16)
            y_out[c, pl.ds(p * SIDE, SIDE)] = got.reshape(SIDE, slots, width)
        send_pairs(y_out, y_in, c, g, z, x, groups, s_y, r_y.at[c])

    def weigh(c, mix):
        wait_bytes(y_in.at[c, pl.ds(0, 2 * groups - 2)], r_y.at[c])
        got = dot(mix[...], y_in[c].reshape(total, width)).astype(BF16)
        sum_out[c] = got.reshape(SIDE, tok, width)

    def add_up(c):
        wait_bytes(sum_in.at[c, pl.ds(0, SIDE - 1)], r_sum.at[c])
        got = sum_in[c, 0].astype(F32)
        for b in range(1, SIDE):
            got = got + sum_in[c, b].astype(F32)
        return got.astype(BF16)

    def step(t, carry):
        @pl.when(t < N_G)
        def _():
            down(3 * t)

            @pl.when(lax.rem(t, 2) == 0)
            def _():
                along_x(out_buf, 3 * t, relay_g, t, g, z, x, s_one, r_one.at[t])

            @pl.when(lax.rem(t, 2) == 1)
            def _():
                along_z(out_buf, 3 * t, relay_g, t, g, z, x, s_one, r_one.at[t])

        @pl.when(t < N_X)
        def _():
            c = 3 * t + 1
            down(c)
            for step in (2, 1, 3):
                peer = ring(z, step)
                remote(out_buf.at[c, peer], mid.at[t, pl.ds(SIDE * z, SIDE)], s_mid.at[0], r_mid.at[t], g, peer, x)
            mid[t, pl.ds(SIDE * z, SIDE)] = out_buf[c, z]

        @pl.when(t < N_Z)
        def _():
            c = 3 * t + 2
            down(c)
            for step in (2, 1, 3):
                peer = ring(x, step)
                remote(
                    out_buf.at[c, :, peer], mid.at[N_X + t, pl.ds(SIDE * x, SIDE)], s_mid.at[1],
                    r_mid.at[N_X + t], g, z, peer,
                )
            for p in range(SIDE):
                mid[N_X + t, SIDE * x + p] = out_buf[c, p, x]

        @pl.when(t == 0)
        def _():
            fill_swap(swap, groups, SIDE * SIDE)

        @pl.when((t >= 1) & (t < N_G + 1))
        def _():
            c = t - 1
            wait_bytes(relay_g.at[c, pl.ds(0, SIDE - 1)], r_one.at[c])

            @pl.when(lax.rem(c, 2) == 0)
            def _():
                along_z(relay_g, c, rows_g, c, g, z, x, s_two, r_two.at[c])

            @pl.when(lax.rem(c, 2) == 1)
            def _():
                along_x(relay_g, c, rows_g, c, g, z, x, s_two, r_two.at[c])

        @pl.when((t >= 1) & (t < N_X + 1))
        def _():
            to_sources(t - 1)

        @pl.when((t >= 1) & (t < N_Z + 1))
        def _():
            to_sources(N_X + t - 1)

        @pl.when((t >= 2) & (t < N_G + 2))
        def _():
            c = t - 2
            wait_bytes(rows_g.at[c, pl.ds(0, SIDE - 1)], r_two.at[c])
            got = dot(mix_g[...], rows_g[c].reshape(total, width)).astype(BF16)
            part_out[c] = got.reshape(groups, seats, width)
            send_groups(part_out, part_in, c, g, z, x, groups, s_last, r_last.at[c])

        @pl.when((t >= 2) & (t < N_X + 2))
        def _():
            c = t - 2
            weigh(c, mix_x)
            for step in (2, 1, 3):
                peer = ring(x, step)
                remote(sum_out.at[c, peer], sum_in.at[c, x], s_sum_x, r_sum.at[c], g, z, peer)
            sum_in[c, x] = sum_out[c, x]

        @pl.when((t >= 2) & (t < N_Z + 2))
        def _():
            c = N_X + t - 2
            weigh(c, mix_z)
            for step in (2, 1, 3):
                peer = ring(z, step)
                remote(sum_out.at[c, peer], sum_in.at[c, z], s_sum_z, r_sum.at[c], g, peer, x)
            sum_in[c, z] = sum_out[c, z]

        @pl.when((t >= 3) & (t < N_G + 3))
        def _():
            c = t - 3
            wait_bytes(part_in.at[c, pl.ds(0, groups - 1)], r_last.at[c])
            out_ref[:, columns(3 * c)] = dot(back_ref[...], part_in[c].reshape(held, width)).astype(BF16)

        @pl.when((t >= 3) & (t < N_X + 3))
        def _():
            out_ref[:, columns(3 * (t - 3) + 1)] = add_up(t - 3)

        @pl.when((t >= 3) & (t < N_Z + 3))
        def _():
            out_ref[:, columns(3 * (t - 3) + 2)] = add_up(N_X + t - 3)

        return carry

    lax.fori_loop(0, N_G + 3, step, 0)
    wait_bytes(relay_g.at[:, pl.ds(0, SIDE - 1)], s_one)
    wait_bytes(rows_g.at[:, pl.ds(0, SIDE - 1)], s_two)
    wait_bytes(mid.at[pl.ds(0, N_X), pl.ds(0, SIDE * (SIDE - 1))], s_mid.at[0])
    wait_bytes(mid.at[pl.ds(N_X, N_Z), pl.ds(0, SIDE * (SIDE - 1))], s_mid.at[1])
    wait_bytes(y_out.at[:, pl.ds(0, 2 * groups - 2)], s_y)
    wait_bytes(part_out.at[:, pl.ds(0, groups - 1)], s_last)
    wait_bytes(sum_out.at[pl.ds(0, N_X), pl.ds(0, SIDE - 1)], s_sum_x)
    wait_bytes(sum_out.at[pl.ds(N_X, N_Z), pl.ds(0, SIDE - 1)], s_sum_z)


def shards(hidden_states, affinity, group_ids, expert_ids, w_gate, w_up, w_down):
    tok, model = hidden_states.shape
    hid = w_gate.shape[2]
    groups = lax.axis_size("group")
    slots = MOST * groups
    seats = tok * TOPG // groups
    held = groups * seats
    total = SIDE * SIDE * slots
    width = model // CHUNKS
    wide = N_X + N_Z

    vmem = pl.BlockSpec(memory_space=pltpu.VMEM)
    anywhere = pl.BlockSpec(memory_space=pl.ANY)
    dma = pltpu.SemaphoreType.DMA

    def grid4(n):
        return pltpu.VMEM((n, SIDE, SIDE, slots, width), BF16)

    def pairs(n):
        return pltpu.VMEM((n, SIDE * SIDE, slots, width), BF16)

    def seated(n, w):
        return pltpu.VMEM((n, groups, seats, w), BF16)

    def spread(n):
        return pltpu.VMEM((n, SIDE, tok, width), BF16)

    mix_shape = jax.ShapeDtypeStruct((held, total), BF16)
    hidden, mix_g, mix_x, mix_z, back = pl.pallas_call(
        functools.partial(dispatch_kernel, groups, slots),
        out_shape=(
            jax.ShapeDtypeStruct((total, hid), BF16), mix_shape, mix_shape, mix_shape,
            jax.ShapeDtypeStruct((tok, held), BF16),
        ),
        in_specs=[vmem, vmem, vmem, vmem, anywhere, anywhere],
        out_specs=(vmem, anywhere, anywhere, anywhere, vmem),
        scratch_shapes=[
            pltpu.VMEM((tok, LANES), BF16),
            pltpu.VMEM((SIDE, tok, LANES), BF16),
            pltpu.VMEM((SIDE, tok, LANES), BF16),
            seated(1, LANES), seated(1, LANES),
            seated(N_G, width), seated(N_G, width),
            spread(N_X), spread(N_Z),
            grid4(N_G), grid4(N_G),
            pairs(wide), pairs(wide),
            grid4(CHUNKS),
            pltpu.VMEM((total, hid), F32),
            pltpu.VMEM((total, hid), F32),
            pltpu.VMEM((2, width, hid), BF16),
            pltpu.VMEM((2, width, hid), BF16),
            pltpu.VMEM((total, held), BF16),
            pltpu.VMEM((total, held), BF16),
            pltpu.VMEM((total, held), BF16),
            pltpu.VMEM((total, total), BF16),
            pltpu.VMEM((held, tok), BF16),
            pltpu.VMEM((held, total), BF16),
            dma((2,)), dma((2,)), dma, dma, dma, dma((N_G,)), dma, dma, dma((wide,)), dma, dma((N_G,)),
            dma, dma((wide,)), dma((wide,)), dma, dma((CHUNKS,)), dma((2, 2)), dma,
        ],
        compiler_params=pltpu.CompilerParams(
            collective_id=0, has_side_effects=True, vmem_limit_bytes=63 * 2**20
        ),
        name="dispatch",
    )(affinity, group_ids, expert_ids, hidden_states, w_gate[0], w_up[0])

    return pl.pallas_call(
        functools.partial(return_kernel, groups, slots),
        out_shape=jax.ShapeDtypeStruct((tok, model), BF16),
        in_specs=[vmem, vmem, vmem, vmem, vmem, anywhere],
        out_specs=vmem,
        scratch_shapes=[
            grid4(CHUNKS), grid4(N_G), grid4(N_G),
            pairs(wide), pairs(wide), pairs(wide),
            seated(N_G, width), seated(N_G, width),
            spread(wide), spread(wide),
            pltpu.VMEM((2, hid, width), BF16),
            pltpu.VMEM((total, total), BF16),
            dma, dma((N_G,)), dma, dma((N_G,)), dma((2,)), dma((wide,)), dma, dma((wide,)),
            dma, dma((N_G,)), dma, dma, dma((wide,)), dma((2,)),
        ],
        compiler_params=pltpu.CompilerParams(
            collective_id=1, has_side_effects=True, vmem_limit_bytes=60 * 2**20
        ),
        name="giveback",
    )(hidden, mix_g, mix_x, mix_z, back, w_down[0])


def solution(mesh):
    placed = (
        P(("group", "local"), None),
        P(("group", "local"), None),
        P(("group", "local"), None),
        P(("group", "local"), None),
        P(("group", "local"), None, None),
        P(("group", "local"), None, None),
        P(("group", "local"), None, None),
    )
    return jax.shard_map(
        shards, mesh=mesh, in_specs=placed, out_specs=P(("group", "local"), None), check_vma=False
    )
```

time: 568 us -> 226 us (0.40)
  the two profiles are of different devices: /device:TPU:28 before, /device:TPU:1 now
where the time goes in v2:
time: 226 us
  Pallas kernels  219 us (97%)
  local copies, waits for them, and re-layouts  6.39 us (3%)
    pallas_call x1, Pallas kernels, shards(): pl.pallas_call(functools.partial(dispatch_kernel, groups, slots), out_sha...  118 us
    pallas_call x1, Pallas kernels, shards(): pl.pallas_call(functools.partial(return_kernel, groups, slots), out_shape...  102 us
    unnamed x4, local copies, waits for them, and re-layouts  6.39 us

profile of v2, /device:TPU:1, one launch (start us, length us, event | category | flops | bytes accessed | tf_op | source)
XLA Modules:
  0.0 225.9 jit_solution(126356201267365989)
XLA Ops:
  0.0 1.4 copy.8.aff_ref
  1.4 1.4 copy.9.gid_ref
  2.8 1.4 copy.10.eid_ref
  4.2 117.6 %dispatch.1 = (bf16[1280,1024]{1,0:T(8,128)(2,1)}, bf16[512,1280]{1,0:T(8,128)(2,1)}, bf16[512,1280]{1,0:T(8,128)(2,1)}, bf16[512,1280]{1,0:T(8,128)(2,1)}, bf16[128,512]{1,0:T(8,128)(2,1)}) custom-call(f32[128,8]{1,0:T(8,128)} %copy.8.aff_ref, s32[128,4]{1,0:T(8,128)} %copy.9.gid_ref, s32[128,8]{1,0:T(8,128)} %copy.10.eid_ref, bf16[128,3584]{1,0:T(8,128)(2,1)} %tok_ref.1, ...), custom_call_target="tpu_custom_call" | custom-call | tf_op jit(solution)/shard_map/dispatch/pallas_call | solution.py:651
  121.8 101.9 %giveback.1 = bf16[128,3584]{1,0:T(8,128)(2,1)} custom-call(bf16[1280,1024]{1,0:T(8,128)(2,1)} %get-tuple-element.10.hid_ref, bf16[512,1280]{1,0:T(8,128)(2,1)} %get-tuple-element.11.mix_g, bf16[512,1280]{1,0:T(8,128)(2,1)} %get-tuple-element.12.mix_x, bf16[512,1280]{1,0:T(8,128)(2,1)} %get-tuple-element.13.mix_z, ...), custom_call_target="tpu_custom_call" | custom-call | tf_op jit(solution)/shard_map/giveback/pallas_call | solution.py:688
  223.7 2.2 copy.12

commit v3 on v2

--- a/solution.py
+++ b/solution.py
@@ -177,7 +177,7 @@
     aff_ref, gid_ref, eid_ref, tok_ref, wg_ref, wu_ref,
     hid_ref, mix_g, mix_x, mix_z, back_ref,
     info_out, info_x, info_z, meta_out, meta_in, first_out, first_in, wide_x, wide_z,
-    out_g, relay_g, y_out, y_in, rows, acc_g, acc_u, wbuf_g, wbuf_u, pick_g, pick_x, pick_z, swap, sel, stage,
+    out_g, relay_g, y_out, y_in, rows, acc_g, acc_u, wbuf_g, wbuf_u, pick_g, pick_x, pick_z, swap, sel, stage, table,
     s_info, r_info, s_meta, r_meta, s_first, r_first, s_wide_x, s_wide_z, r_wide, s_one, r_one,
     s_two, s_y, r_y, s_end, r_rows, w_sem, mix_sem,
 ):
@@ -205,22 +205,18 @@
             cp.start()
 
     aff = aff_ref[...]
-    scaled = (2.5 * aff / jnp.sum(aff, axis=1, keepdims=True)).astype(BF16)
+    scaled = (2.5 * aff / jnp.sum(aff, axis=0, keepdims=True)).astype(BF16).astype(F32)
     gid = gid_ref[...].astype(F32)
     eid = eid_ref[...].astype(F32)
-    twice = one_hot(jnp.floor(iota((TOPG, TOP_K), 1) / 2.0) == iota((TOPG, TOP_K), 0))
-    chosen = dot(gid.astype(BF16), twice)
     owner = jnp.floor(eid / float(local))
+    chosen = jnp.concatenate([gid[k // 2 : k // 2 + 1, :] for k in range(TOP_K)], axis=0)
     is_valid = owner == chosen
-    mixing = jnp.where(is_valid, scaled.astype(F32), 0.0).astype(BF16)
-    inside = jnp.where(is_valid, eid - float(local) * owner, -1.0).astype(BF16)
-    lane_of = iota((TOP_K, LANES), 1) - iota((TOP_K, LANES), 0)
-    lane_of4 = iota((TOPG, LANES), 1) - iota((TOPG, LANES), 0)
-    rt = (
-        dot(inside, one_hot(lane_of == 0.0))
-        + dot(mixing, one_hot(lane_of == float(TOP_K)))
-        + dot(gid.astype(BF16), one_hot(lane_of4 == float(2 * TOP_K)))
+    mixing = jnp.where(is_valid, scaled, 0.0)
+    inside = jnp.where(is_valid, eid - float(local) * owner, -1.0)
+    rt_t = jnp.concatenate(
+        [inside, mixing, gid, jnp.zeros((LANES - 2 * TOP_K - TOPG, tok), F32)], axis=0
     )
+    rt = jnp.transpose(rt_t)
     info_out[...] = rt.astype(BF16)
     info_x[x] = info_out[...]
     info_z[z] = info_out[...]
@@ -232,7 +228,6 @@
         peer = ring(z, step)
         remote(info_out, info_z.at[z], s_info.at[1], r_info.at[1], g, peer, x)
 
-    rt_t = jnp.transpose(rt)
     group_at = iota((groups, tok), 0)
     member = jnp.zeros((groups, tok), F32)
     for j in range(TOPG):
@@ -263,22 +258,40 @@
 
     lax.fori_loop(0, N_G, first, 0)
 
-    row = iota((2 * local, held), 0)
-    wait_bytes(info_x.at[pl.ds(0, SIDE - 1)], r_info.at[0])
-    ids, mixes = read_info(jnp.transpose(info_x[...].reshape(held, LANES).astype(F32)))
-    seat_x, weight_x = rank_table(ids, mixes, row * float(SIDE) + x.astype(F32), float(tok))
-    fill_pick(pick_x, seat_x, float(SIDE * MOST), float(SIDE), float(tok))
-    wait_bytes(meta_in.at[0, pl.ds(0, groups - 1)], r_meta)
-    ids, mixes = read_info(jnp.transpose(meta_in[0].reshape(held, LANES).astype(F32)))
-    seat_g, weight_g = rank_table(
-        ids, mixes, iota((local, held), 0) + float(local) * g.astype(F32), float(seats)
-    )
-    fill_pick(pick_g, seat_g, float(slots), float(groups), float(seats))
-    wait_bytes(info_z.at[pl.ds(0, SIDE - 1)], r_info.at[1])
-    ids, mixes = read_info(jnp.transpose(info_z[...].reshape(held, LANES).astype(F32)))
-    own = jnp.floor(row / float(SIDE)) * float(local - SIDE) + row + float(SIDE) * z.astype(F32)
-    seat_z, weight_z = rank_table(ids, mixes, own, float(tok))
-    fill_pick(pick_z, seat_z, float(SIDE * MOST), float(SIDE), float(tok))
+    def clear(b, carry):
+        at = pl.ds(pl.multiple_of(b * slots, slots), slots)
+        acc_g[at, :] = jnp.zeros((slots, acc_g.shape[1]), F32)
+        acc_u[at, :] = jnp.zeros((slots, acc_u.shape[1]), F32)
+        return carry
+
+    lax.fori_loop(0, total // slots, clear, 0)
+
+    def plan_g():
+        wait_bytes(meta_in.at[0, pl.ds(0, groups - 1)], r_meta)
+        ids, mixes = read_info(jnp.transpose(meta_in[0].reshape(held, LANES).astype(F32)))
+        own = iota((local, held), 0) + float(local) * g.astype(F32)
+        seat_in, weight = rank_table(ids, mixes, own, float(seats))
+        fill_pick(pick_g, seat_in, float(slots), float(groups), float(seats))
+        table[0, 0:local, :] = seat_in
+        table[0, local : 2 * local, :] = weight
+
+    def plan_wide(info, which, own, pick):
+        wait_bytes(info.at[pl.ds(0, SIDE - 1)], r_info.at[which])
+        ids, mixes = read_info(jnp.transpose(info[...].reshape(held, LANES).astype(F32)))
+        seat_in, weight = rank_table(ids, mixes, own, float(tok))
+        fill_pick(pick, seat_in, float(SIDE * MOST), float(SIDE), float(tok))
+        table[1 + which, 0 : 2 * local, :] = seat_in
+        table[1 + which, 2 * local : 4 * local, :] = weight
+
+    def plan_x():
+        plan_wide(info_x, 0, iota((2 * local, held), 0) * float(SIDE) + x.astype(F32), pick_x)
+
+    def plan_z():
+        row = iota((2 * local, held), 0)
+        own = jnp.floor(row / float(SIDE)) * float(local - SIDE) + row + float(SIDE) * z.astype(F32)
+        plan_wide(info_z, 1, own, pick_z)
+
+    plan_g()
 
     def to_peers(c, src, pick):
         for p in range(SIDE):
@@ -311,10 +324,14 @@
             def _():
                 along_z(out_g, t, relay_g, t, g, z, x, s_one, r_one.at[t])
 
+        pl.when(t == 0)(plan_x)
+
         @pl.when(t < N_X)
         def _():
             wait_bytes(wide_x.at[t, pl.ds(0, SIDE - 1)], r_wide.at[t])
             to_peers(t, wide_x[t].reshape(held, width), pick_x)
+
+        pl.when(t == 0)(plan_z)
 
         @pl.when(t < N_Z)
         def _():
@@ -370,11 +387,11 @@
                 put.start()
                 put.wait()
 
-            fill_mix(stage, seat_g, weight_g, float(slots), float(groups), float(seats))
+            fill_mix(stage, table[0, 0:local, :], table[0, local : 2 * local, :], float(slots), float(groups), float(seats))
             keep(mix_g)
-            fill_mix(stage, seat_x, weight_x, float(SIDE * MOST), float(SIDE), float(tok))
+            fill_mix(stage, table[1, 0 : 2 * local, :], table[1, 2 * local : 4 * local, :], float(SIDE * MOST), float(SIDE), float(tok))
             keep(mix_x)
-            fill_mix(stage, seat_z, weight_z, float(SIDE * MOST), float(SIDE), float(tok))
+            fill_mix(stage, table[2, 0 : 2 * local, :], table[2, 2 * local : 4 * local, :], float(SIDE * MOST), float(SIDE), float(tok))
             keep(mix_z)
             seat_t = jnp.transpose(jnp.concatenate([seat, jnp.full((tok - groups, tok), -1.0, F32)], axis=0))
             lane_at = iota((tok, held), 1)
@@ -394,19 +411,8 @@
             def piece(p, inner):
                 at = pl.ds(pl.multiple_of(p * block, block), block)
                 part = rows[c, p].reshape(block, width)
-                got_g = dot(part, wbuf_g[slot])
-                got_u = dot(part, wbuf_u[slot])
-
-                @pl.when(c == 0)
-                def _():
-                    acc_g[at, :] = got_g
-                    acc_u[at, :] = got_u
-
-                @pl.when(c > 0)
-                def _():
-                    acc_g[at, :] = acc_g[at, :] + got_g
-                    acc_u[at, :] = acc_u[at, :] + got_u
-
+                acc_g[at, :] += dot(part, wbuf_g[slot])
+                acc_u[at, :] += dot(part, wbuf_u[slot])
                 return inner
 
             lax.fori_loop(0, SIDE, piece, 0)
@@ -447,10 +453,10 @@
 
 def return_kernel(
     groups, slots,
-    hid_ref, mix_g, mix_x, mix_z, back_ref, wd_ref,
+    hid_ref, mix_hbm_g, mix_hbm_x, mix_hbm_z, back_ref, wd_ref,
     out_ref,
-    out_buf, relay_g, rows_g, mid, y_out, y_in, part_out, part_in, sum_out, sum_in, wbuf, swap,
-    s_one, r_one, s_two, r_two, s_mid, r_mid, s_y, r_y, s_last, r_last, s_sum_x, s_sum_z, r_sum, w_sem,
+    out_buf, relay_g, rows_g, mid, y_out, y_in, part_out, part_in, sum_out, sum_in, wbuf, swap, mix_g, mix_x, mix_z,
+    s_one, r_one, s_two, r_two, s_mid, r_mid, s_y, r_y, s_last, r_last, s_sum_x, s_sum_z, r_sum, w_sem, mix_sem,
 ):
     g, z, x = position()
     tok = out_ref.shape[0]
@@ -470,6 +476,11 @@
     for c in range(2):
         weights(c).start()
     entry_barrier(g, z, x, groups)
+    mixes = [
+        pltpu.make_async_copy(mix_hbm_g, mix_g, mix_sem.at[0]),
+        pltpu.make_async_copy(mix_hbm_x, mix_x, mix_sem.at[1]),
+        pltpu.make_async_copy(mix_hbm_z, mix_z, mix_sem.at[2]),
+    ]
 
     def down(c):
         slot = lax.rem(c, 2)
@@ -544,7 +555,11 @@
 
         @pl.when(t == 0)
         def _():
+            for cp in mixes:
+                cp.start()
             fill_swap(swap, groups, SIDE * SIDE)
+            for cp in mixes:
+                cp.wait()
 
         @pl.when((t >= 1) & (t < N_G + 1))
         def _():
@@ -676,6 +691,7 @@
             pltpu.VMEM((total, total), BF16),
             pltpu.VMEM((held, tok), BF16),
             pltpu.VMEM((held, total), BF16),
+            pltpu.VMEM((3, LANES, held), F32),
             dma((2,)), dma((2,)), dma, dma, dma, dma((N_G,)), dma, dma, dma((wide,)), dma, dma((N_G,)),
             dma, dma((wide,)), dma((wide,)), dma, dma((CHUNKS,)), dma((2, 2)), dma,
         ],
@@ -683,12 +699,12 @@
             collective_id=0, has_side_effects=True, vmem_limit_bytes=63 * 2**20
         ),
         name="dispatch",
-    )(affinity, group_ids, expert_ids, hidden_states, w_gate[0], w_up[0])
+    )(affinity.T, group_ids.T, expert_ids.T, hidden_states, w_gate[0], w_up[0])
 
     return pl.pallas_call(
         functools.partial(return_kernel, groups, slots),
         out_shape=jax.ShapeDtypeStruct((tok, model), BF16),
-        in_specs=[vmem, vmem, vmem, vmem, vmem, anywhere],
+        in_specs=[vmem, anywhere, anywhere, anywhere, vmem, anywhere],
         out_specs=vmem,
         scratch_shapes=[
             grid4(CHUNKS), grid4(N_G), grid4(N_G),
@@ -697,8 +713,11 @@
             spread(wide), spread(wide),
             pltpu.VMEM((2, hid, width), BF16),
             pltpu.VMEM((total, total), BF16),
+            pltpu.VMEM((held, total), BF16),
+            pltpu.VMEM((held, total), BF16),
+            pltpu.VMEM((held, total), BF16),
             dma, dma((N_G,)), dma, dma((N_G,)), dma((2,)), dma((wide,)), dma, dma((wide,)),
-            dma, dma((N_G,)), dma, dma, dma((wide,)), dma((2,)),
+            dma, dma((N_G,)), dma, dma, dma((wide,)), dma((2,)), dma((3,)),
         ],
         compiler_params=pltpu.CompilerParams(
             collective_id=1, has_side_effects=True, vmem_limit_bytes=60 * 2**20

time: 226 us -> 215 us (0.951)
  Pallas kernels: 219 us -> 213 us
  local copies, waits for them, and re-layouts: 6.39 us -> 2.16 us
    unnamed x4 -> x1, local copies, waits for them, and re-layouts: 6.39 us -> 2.16 us
    pallas_call x1, Pallas kernels: 118 us -> 113 us  [shards(): pl.pallas_call(functools.partial(dispatch_kernel, groups, slots), out_sha...]
    pallas_call x1, Pallas kernels: 102 us -> 99.3 us  [shards(): pl.pallas_call(functools.partial(return_kernel, groups, slots), out_shape...]
where the time goes in v3:
time: 215 us
  Pallas kernels  213 us (99%)
  local copies, waits for them, and re-layouts  2.16 us (1%)
    pallas_call x1, Pallas kernels, shards(): pl.pallas_call(functools.partial(dispatch_kernel, groups, slots), out_sha...  113 us
    pallas_call x1, Pallas kernels, shards(): pl.pallas_call(functools.partial(return_kernel, groups, slots), out_shape...  99.3 us

profile of v3, /device:TPU:1, one launch (start us, length us, event | category | flops | bytes accessed | tf_op | source)
XLA Modules:
  0.0 214.9 jit_solution(7232914894409822082)
XLA Ops:
  0.0 113.4 %dispatch.1 = (bf16[1280,1024]{1,0:T(8,128)(2,1)}, bf16[512,1280]{1,0:T(8,128)(2,1)}, bf16[512,1280]{1,0:T(8,128)(2,1)}, bf16[512,1280]{1,0:T(8,128)(2,1)}, bf16[128,512]{1,0:T(8,128)(2,1)}) custom-call(f32[8,128]{1,0:T(8,128)} %bitcast.9, s32[4,128]{1,0:T(4,128)} %bitcast.11, s32[8,128]{1,0:T(8,128)} %bitcast.10, bf16[128,3584]{1,0:T(8,128)(2,1)} %tok_ref.1, ...), custom_call_target="tpu_custom_call" | custom-call | tf_op jit(solution)/shard_map/dispatch/pallas_call | solution.py:666
  113.4 99.3 %giveback.1 = bf16[128,3584]{1,0:T(8,128)(2,1)} custom-call(bf16[1280,1024]{1,0:T(8,128)(2,1)} %get-tuple-element.10.hid_ref, bf16[512,1280]{1,0:T(8,128)(2,1)} %get-tuple-element.11.mix_hbm_g, bf16[512,1280]{1,0:T(8,128)(2,1)} %get-tuple-element.12.mix_hbm_x, bf16[512,1280]{1,0:T(8,128)(2,1)} %get-tuple-element.13.mix_hbm_z, ...), custom_call_target="tpu_custom_call" | custom-call | tf_op jit(solution)/shard_map/giveback/pallas_call | solution.py:704
  212.7 2.2 %copy.9 = bf16[128,3584]{1,0:T(8,128)(2,1)} copy(bf16[128,3584]{1,0:T(8,128)(2,1)} %giveback.1) | data formatting | bytes 1835008

commit v4 on v3

--- a/solution.py
+++ b/solution.py
@@ -12,8 +12,8 @@
 SIDE = 4
 MOST = 10
 CHUNKS = 14
-N_G = 5
-N_X = 5
+N_G = 6
+N_X = 4
 N_Z = 4
 LANES = 128
 MESH = pl.DeviceIdType.MESH
@@ -193,6 +193,15 @@
     def columns(c):
         return pl.ds(pl.multiple_of(c * width, width), width)
 
+    def group_at_step(t):
+        return jnp.minimum(2 * t, t + 2)
+
+    def step_column(t):
+        return jnp.minimum(4 * t, 3 * t + 2)
+
+    def group_column(k):
+        return k // 2 * 4 + k % 2 + 2 * (k // 5)
+
     def weights(c):
         slot = lax.rem(c, 2)
         return (
@@ -241,16 +250,16 @@
     send_groups(meta_out, meta_in, 0, g, z, x, groups, s_meta, r_meta)
 
     def first(t, carry):
-        got = dot(sel[...], tok_ref[:, columns(3 * t)]).astype(BF16)
+        got = dot(sel[...], tok_ref[:, columns(group_column(t))]).astype(BF16)
         first_out[t] = got.reshape(groups, seats, width)
         send_groups(first_out, first_in, t, g, z, x, groups, s_first, r_first.at[t])
-        wide_x[t, x] = tok_ref[:, columns(3 * t + 1)]
-        for step in (2, 1, 3):
-            remote(wide_x.at[t, x], wide_x.at[t, x], s_wide_x, r_wide.at[t], g, z, ring(x, step))
-
-        @pl.when(t < N_Z)
-        def _():
-            wide_z[t, z] = tok_ref[:, columns(3 * t + 2)]
+
+        @pl.when(t < N_X)
+        def _():
+            wide_x[t, x] = tok_ref[:, columns(step_column(t + 1) - 2)]
+            for step in (2, 1, 3):
+                remote(wide_x.at[t, x], wide_x.at[t, x], s_wide_x, r_wide.at[t], g, z, ring(x, step))
+            wide_z[t, z] = tok_ref[:, columns(step_column(t + 1) - 1)]
             for step in (2, 1, 3):
                 remote(wide_z.at[t, z], wide_z.at[t, z], s_wide_z, r_wide.at[N_X + t], g, ring(z, step), x)
 
@@ -308,21 +317,26 @@
             y_out[c, pl.ds(p * SIDE, SIDE)] = got.reshape(SIDE, slots, width)
 
     def step(t, carry):
-        @pl.when(t < N_G)
-        def _():
-            wait_bytes(first_in.at[t, pl.ds(0, groups - 1)], r_first.at[t])
-            src = first_in[t].reshape(held, width)
+        def spread_group(k, inner):
+            wait_bytes(first_in.at[k, pl.ds(0, groups - 1)], r_first.at[k])
+            src = first_in[k].reshape(held, width)
             for p in range(SIDE):
                 got = dot(pick_g[p * block : (p + 1) * block, :], src).astype(BF16)
-                out_g[t, p] = got.reshape(SIDE, slots, width)
-
-            @pl.when(lax.rem(t, 2) == 0)
-            def _():
-                along_x(out_g, t, relay_g, t, g, z, x, s_one, r_one.at[t])
-
-            @pl.when(lax.rem(t, 2) == 1)
-            def _():
-                along_z(out_g, t, relay_g, t, g, z, x, s_one, r_one.at[t])
+                out_g[k, p] = got.reshape(SIDE, slots, width)
+
+            @pl.when(lax.rem(k, 2) == 0)
+            def _():
+                along_x(out_g, k, relay_g, k, g, z, x, s_one, r_one.at[k])
+
+            @pl.when(lax.rem(k, 2) == 1)
+            def _():
+                along_z(out_g, k, relay_g, k, g, z, x, s_one, r_one.at[k])
+
+            return inner
+
+        @pl.when(t < N_X)
+        def _():
+            lax.fori_loop(group_at_step(t), group_at_step(t + 1), spread_group, 0)
 
         pl.when(t == 0)(plan_x)
 
@@ -342,18 +356,22 @@
         def _():
             fill_swap(swap, local, groups)
 
-        @pl.when((t >= 1) & (t < N_G + 1))
-        def _():
-            c = t - 1
-            wait_bytes(relay_g.at[c, pl.ds(0, SIDE - 1)], r_one.at[c])
-
-            @pl.when(lax.rem(c, 2) == 0)
-            def _():
-                along_z(relay_g, c, rows, 3 * c, g, z, x, s_two, r_rows.at[3 * c])
-
-            @pl.when(lax.rem(c, 2) == 1)
-            def _():
-                along_x(relay_g, c, rows, 3 * c, g, z, x, s_two, r_rows.at[3 * c])
+        def pass_group(k, inner):
+            wait_bytes(relay_g.at[k, pl.ds(0, SIDE - 1)], r_one.at[k])
+
+            @pl.when(lax.rem(k, 2) == 0)
+            def _():
+                along_z(relay_g, k, rows, group_column(k), g, z, x, s_two, r_rows.at[group_column(k)])
+
+            @pl.when(lax.rem(k, 2) == 1)
+            def _():
+                along_x(relay_g, k, rows, group_column(k), g, z, x, s_two, r_rows.at[group_column(k)])
+
+            return inner
+
+        @pl.when((t >= 1) & (t < N_X + 1))
+        def _():
+            lax.fori_loop(group_at_step(t - 1), group_at_step(t), pass_group, 0)
 
         @pl.when((t >= 1) & (t < N_X + 1))
         def _():
@@ -362,10 +380,10 @@
             for step in (2, 1, 3):
                 peer = ring(z, step)
                 remote(
-                    y_out.at[c, pl.ds(SIDE * peer, SIDE)], rows.at[3 * c + 1, z], s_end, r_rows.at[3 * c + 1],
+                    y_out.at[c, pl.ds(SIDE * peer, SIDE)], rows.at[step_column(t) - 2, z], s_end, r_rows.at[step_column(t) - 2],
                     g, peer, x,
                 )
-            rows[3 * c + 1, z] = y_out[c, pl.ds(SIDE * z, SIDE)]
+            rows[step_column(t) - 2, z] = y_out[c, pl.ds(SIDE * z, SIDE)]
 
         @pl.when((t >= 1) & (t < N_Z + 1))
         def _():
@@ -374,11 +392,11 @@
             for step in (2, 1, 3):
                 peer = ring(x, step)
                 remote(
-                    y_out.at[N_X + c, pl.ds(SIDE * peer, SIDE)], rows.at[3 * c + 2, :, x], s_end,
-                    r_rows.at[3 * c + 2], g, z, peer,
+                    y_out.at[N_X + c, pl.ds(SIDE * peer, SIDE)], rows.at[step_column(t) - 1, :, x], s_end,
+                    r_rows.at[step_column(t) - 1], g, z, peer,
                 )
             for p in range(SIDE):
-                rows[3 * c + 2, p, x] = y_out[N_X + c, SIDE * x + p]
+                rows[step_column(t) - 1, p, x] = y_out[N_X + c, SIDE * x + p]
 
         @pl.when(t == 1)
         def _():
@@ -426,12 +444,12 @@
 
         @pl.when(t >= 2)
         def _():
-            low = 3 * (t - 2)
-            lax.fori_loop(low, jnp.minimum(low + 3, CHUNKS), multiply, 0)
+            c = t - 2
+            lax.fori_loop(step_column(c), step_column(c + 1), multiply, 0)
 
         return carry
 
-    lax.fori_loop(0, N_G + 2, step, 0)
+    lax.fori_loop(0, N_X + 2, step, 0)
 
     def finish(b, carry):
         at = pl.ds(pl.multiple_of(b * slots, slots), slots)
@@ -469,6 +487,15 @@
     def columns(c):
         return pl.ds(pl.multiple_of(c * width, width), width)
 
+    def group_at_step(t):
+        return jnp.maximum(jnp.minimum(2 * t - 1, t + 2), 0)
+
+    def step_column(t):
+        return 2 * t + group_at_step(t)
+
+    def group_column(k):
+        return 2 * ((k + 1) // 2) + 2 + k
+
     def weights(c):
         slot = lax.rem(c, 2)
         return pltpu.make_async_copy(wd_ref.at[:, columns(c)], wbuf.at[slot], w_sem.at[slot])
@@ -519,21 +546,9 @@
         return got.astype(BF16)
 
     def step(t, carry):
-        @pl.when(t < N_G)
-        def _():
-            down(3 * t)
-
-            @pl.when(lax.rem(t, 2) == 0)
-            def _():
-                along_x(out_buf, 3 * t, relay_g, t, g, z, x, s_one, r_one.at[t])
-
-            @pl.when(lax.rem(t, 2) == 1)
-            def _():
-                along_z(out_buf, 3 * t, relay_g, t, g, z, x, s_one, r_one.at[t])
-
         @pl.when(t < N_X)
         def _():
-            c = 3 * t + 1
+            c = step_column(t)
             down(c)
             for step in (2, 1, 3):
                 peer = ring(z, step)
@@ -542,7 +557,7 @@
 
         @pl.when(t < N_Z)
         def _():
-            c = 3 * t + 2
+            c = step_column(t) + 1
             down(c)
             for step in (2, 1, 3):
                 peer = ring(x, step)
@@ -553,6 +568,24 @@
             for p in range(SIDE):
                 mid[N_X + t, SIDE * x + p] = out_buf[c, p, x]
 
+        def start_group(k, inner):
+            c = group_column(k)
+            down(c)
+
+            @pl.when(lax.rem(k, 2) == 0)
+            def _():
+                along_x(out_buf, c, relay_g, k, g, z, x, s_one, r_one.at[k])
+
+            @pl.when(lax.rem(k, 2) == 1)
+            def _():
+                along_z(out_buf, c, relay_g, k, g, z, x, s_one, r_one.at[k])
+
+            return inner
+
+        @pl.when(t < N_X)
+        def _():
+            lax.fori_loop(group_at_step(t), group_at_step(t + 1), start_group, 0)
+
         @pl.when(t == 0)
         def _():
             for cp in mixes:
@@ -561,19 +594,6 @@
             for cp in mixes:
                 cp.wait()
 
-        @pl.when((t >= 1) & (t < N_G + 1))
-        def _():
-            c = t - 1
-            wait_bytes(relay_g.at[c, pl.ds(0, SIDE - 1)], r_one.at[c])
-
-            @pl.when(lax.rem(c, 2) == 0)
-            def _():
-                along_z(relay_g, c, rows_g, c, g, z, x, s_two, r_two.at[c])
-
-            @pl.when(lax.rem(c, 2) == 1)
-            def _():
-                along_x(relay_g, c, rows_g, c, g, z, x, s_two, r_two.at[c])
-
         @pl.when((t >= 1) & (t < N_X + 1))
         def _():
             to_sources(t - 1)
@@ -582,13 +602,22 @@
         def _():
             to_sources(N_X + t - 1)
 
-        @pl.when((t >= 2) & (t < N_G + 2))
-        def _():
-            c = t - 2
-            wait_bytes(rows_g.at[c, pl.ds(0, SIDE - 1)], r_two.at[c])
-            got = dot(mix_g[...], rows_g[c].reshape(total, width)).astype(BF16)
-            part_out[c] = got.reshape(groups, seats, width)
-            send_groups(part_out, part_in, c, g, z, x, groups, s_last, r_last.at[c])
+        def pass_group(k, inner):
+            wait_bytes(relay_g.at[k, pl.ds(0, SIDE - 1)], r_one.at[k])
+
+            @pl.when(lax.rem(k, 2) == 0)
+            def _():
+                along_z(relay_g, k, rows_g, k, g, z, x, s_two, r_two.at[k])
+
+            @pl.when(lax.rem(k, 2) == 1)
+            def _():
+                along_x(relay_g, k, rows_g, k, g, z, x, s_two, r_two.at[k])
+
+            return inner
+
+        @pl.when((t >= 1) & (t < N_X + 1))
+        def _():
+            lax.fori_loop(group_at_step(t - 1), group_at_step(t), pass_group, 0)
 
         @pl.when((t >= 2) & (t < N_X + 2))
         def _():
@@ -608,23 +637,37 @@
                 remote(sum_out.at[c, peer], sum_in.at[c, z], s_sum_z, r_sum.at[c], g, peer, x)
             sum_in[c, z] = sum_out[c, z]
 
-        @pl.when((t >= 3) & (t < N_G + 3))
-        def _():
-            c = t - 3
-            wait_bytes(part_in.at[c, pl.ds(0, groups - 1)], r_last.at[c])
-            out_ref[:, columns(3 * c)] = dot(back_ref[...], part_in[c].reshape(held, width)).astype(BF16)
+        def weigh_group(k, inner):
+            wait_bytes(rows_g.at[k, pl.ds(0, SIDE - 1)], r_two.at[k])
+            got = dot(mix_g[...], rows_g[k].reshape(total, width)).astype(BF16)
+            part_out[k] = got.reshape(groups, seats, width)
+            send_groups(part_out, part_in, k, g, z, x, groups, s_last, r_last.at[k])
+            return inner
+
+        @pl.when((t >= 2) & (t < N_X + 2))
+        def _():
+            lax.fori_loop(group_at_step(t - 2), group_at_step(t - 1), weigh_group, 0)
+
+        def place_group(k, inner):
+            wait_bytes(part_in.at[k, pl.ds(0, groups - 1)], r_last.at[k])
+            out_ref[:, columns(group_column(k))] = dot(back_ref[...], part_in[k].reshape(held, width)).astype(BF16)
+            return inner
 
         @pl.when((t >= 3) & (t < N_X + 3))
         def _():
-            out_ref[:, columns(3 * (t - 3) + 1)] = add_up(t - 3)
+            lax.fori_loop(group_at_step(t - 3), group_at_step(t - 2), place_group, 0)
+
+        @pl.when((t >= 3) & (t < N_X + 3))
+        def _():
+            out_ref[:, columns(step_column(t - 3))] = add_up(t - 3)
 
         @pl.when((t >= 3) & (t < N_Z + 3))
         def _():
-            out_ref[:, columns(3 * (t - 3) + 2)] = add_up(N_X + t - 3)
+            out_ref[:, columns(step_column(t - 3) + 1)] = add_up(N_X + t - 3)
 
         return carry
 
-    lax.fori_loop(0, N_G + 3, step, 0)
+    lax.fori_loop(0, N_X + 3, step, 0)
     wait_bytes(relay_g.at[:, pl.ds(0, SIDE - 1)], s_one)
     wait_bytes(rows_g.at[:, pl.ds(0, SIDE - 1)], s_two)
     wait_bytes(mid.at[pl.ds(0, N_X), pl.ds(0, SIDE * (SIDE - 1))], s_mid.at[0])

time: 215 us -> 203 us (0.944)
  Pallas kernels: 213 us -> 201 us
    pallas_call x1, Pallas kernels: 113 us -> 107 us  [shards(): pl.pallas_call(functools.partial(dispatch_kernel, groups, slots), out_sha...]
    pallas_call x1, Pallas kernels: 99.3 us -> 94 us  [shards(): pl.pallas_call(functools.partial(return_kernel, groups, slots), out_shape...]
where the time goes in v4:
time: 203 us
  Pallas kernels  201 us (99%)
  local copies, waits for them, and re-layouts  2.16 us (1%)
    pallas_call x1, Pallas kernels, shards(): pl.pallas_call(functools.partial(dispatch_kernel, groups, slots), out_sha...  107 us
    pallas_call x1, Pallas kernels, shards(): pl.pallas_call(functools.partial(return_kernel, groups, slots), out_shape...  94 us

profile of v4, /device:TPU:1, one launch (start us, length us, event | category | flops | bytes accessed | tf_op | source)
XLA Modules:
  0.0 202.8 jit_solution(5956222236008342792)
XLA Ops:
  0.0 106.6 %dispatch.1 = (bf16[1280,1024]{1,0:T(8,128)(2,1)}, bf16[512,1280]{1,0:T(8,128)(2,1)}, bf16[512,1280]{1,0:T(8,128)(2,1)}, bf16[512,1280]{1,0:T(8,128)(2,1)}, bf16[128,512]{1,0:T(8,128)(2,1)}) custom-call(f32[8,128]{1,0:T(8,128)} %bitcast.9, s32[4,128]{1,0:T(4,128)} %bitcast.11, s32[8,128]{1,0:T(8,128)} %bitcast.10, bf16[128,3584]{1,0:T(8,128)(2,1)} %tok_ref.1, ...), custom_call_target="tpu_custom_call" | custom-call | tf_op jit(solution)/shard_map/dispatch/pallas_call | solution.py:709
  106.6 94.0 %giveback.1 = bf16[128,3584]{1,0:T(8,128)(2,1)} custom-call(bf16[1280,1024]{1,0:T(8,128)(2,1)} %get-tuple-element.10.hid_ref, bf16[512,1280]{1,0:T(8,128)(2,1)} %get-tuple-element.11.mix_hbm_g, bf16[512,1280]{1,0:T(8,128)(2,1)} %get-tuple-element.12.mix_hbm_x, bf16[512,1280]{1,0:T(8,128)(2,1)} %get-tuple-element.13.mix_hbm_z, ...), custom_call_target="tpu_custom_call" | custom-call | tf_op jit(solution)/shard_map/giveback/pallas_call | solution.py:747
  200.7 2.2 %copy.9 = bf16[128,3584]{1,0:T(8,128)(2,1)} copy(bf16[128,3584]{1,0:T(8,128)(2,1)} %giveback.1) | data formatting | bytes 1835008

commit v5 on v4

--- a/solution.py
+++ b/solution.py
@@ -63,10 +63,12 @@
         pl.semaphore_signal(sem, inc=1, device_id=(g, z * SIDE + ring(x, step)), device_id_type=MESH)
 
 
-def entry_barrier(g, z, x, groups):
-    bar = pltpu.get_barrier_semaphore()
-    signal_peers(bar, g, z, x, groups)
-    pl.semaphore_wait(bar, groups - 1 + 2 * (SIDE - 1))
+def barrier_signal(g, z, x, groups):
+    signal_peers(pltpu.get_barrier_semaphore(), g, z, x, groups)
+
+
+def barrier_wait(groups):
+    pl.semaphore_wait(pltpu.get_barrier_semaphore(), groups - 1 + 2 * (SIDE - 1))
 
 
 def send_groups(src, dst, c, g, z, x, groups, ssem, rsem):
@@ -182,6 +184,7 @@
     s_two, s_y, r_y, s_end, r_rows, w_sem, mix_sem,
 ):
     g, z, x = position()
+    barrier_signal(g, z, x, groups)
     tok = tok_ref.shape[0]
     width = tok_ref.shape[1] // CHUNKS
     seats = tok * TOPG // groups
@@ -230,7 +233,7 @@
     info_x[x] = info_out[...]
     info_z[z] = info_out[...]
 
-    entry_barrier(g, z, x, groups)
+    barrier_wait(groups)
     for step in (2, 1, 3):
         peer = ring(x, step)
         remote(info_out, info_x.at[x], s_info.at[0], r_info.at[0], g, z, peer)
@@ -477,6 +480,7 @@
     s_one, r_one, s_two, r_two, s_mid, r_mid, s_y, r_y, s_last, r_last, s_sum_x, s_sum_z, r_sum, w_sem, mix_sem,
 ):
     g, z, x = position()
+    barrier_signal(g, z, x, groups)
     tok = out_ref.shape[0]
     width = out_ref.shape[1] // CHUNKS
     held = mix_g.shape[0]
@@ -502,7 +506,6 @@
 
     for c in range(2):
         weights(c).start()
-    entry_barrier(g, z, x, groups)
     mixes = [
         pltpu.make_async_copy(mix_hbm_g, mix_g, mix_sem.at[0]),
         pltpu.make_async_copy(mix_hbm_x, mix_x, mix_sem.at[1]),
@@ -524,6 +527,9 @@
         @pl.when(c + 2 < CHUNKS)
         def _():
             weights(c + 2).start()
+
+    down(0)
+    barrier_wait(groups)
 
     def to_sources(c):
         wait_bytes(mid.at[c, pl.ds(0, SIDE * (SIDE - 1))], r_mid.at[c])
@@ -549,7 +555,11 @@
         @pl.when(t < N_X)
         def _():
             c = step_column(t)
-            down(c)
+
+            @pl.when(t > 0)
+            def _():
+                down(c)
+
             for step in (2, 1, 3):
                 peer = ring(z, step)
                 remote(out_buf.at[c, peer], mid.at[t, pl.ds(SIDE * z, SIDE)], s_mid.at[0], r_mid.at[t], g, peer, x)

time: 203 us -> 202 us (level)
  no operation moved by 1% of the time
where the time goes in v5:
time: 202 us
  Pallas kernels  200 us (99%)
  local copies, waits for them, and re-layouts  2.16 us (1%)
    pallas_call x1, Pallas kernels, shards(): pl.pallas_call(functools.partial(dispatch_kernel, groups, slots), out_sha...  106 us
    pallas_call x1, Pallas kernels, shards(): pl.pallas_call(functools.partial(return_kernel, groups, slots), out_shape...  93.4 us

profile of v5, /device:TPU:1, one launch (start us, length us, event | category | flops | bytes accessed | tf_op | source)
XLA Modules:
  0.0 202.0 jit_solution(1057876211119169000)
XLA Ops:
  0.0 106.4 %dispatch.1 = (bf16[1280,1024]{1,0:T(8,128)(2,1)}, bf16[512,1280]{1,0:T(8,128)(2,1)}, bf16[512,1280]{1,0:T(8,128)(2,1)}, bf16[512,1280]{1,0:T(8,128)(2,1)}, bf16[128,512]{1,0:T(8,128)(2,1)}) custom-call(f32[8,128]{1,0:T(8,128)} %bitcast.9, s32[4,128]{1,0:T(4,128)} %bitcast.11, s32[8,128]{1,0:T(8,128)} %bitcast.10, bf16[128,3584]{1,0:T(8,128)(2,1)} %tok_ref.1, ...), custom_call_target="tpu_custom_call" | custom-call | tf_op jit(solution)/shard_map/dispatch/pallas_call | solution.py:719
  106.4 93.4 %giveback.1 = bf16[128,3584]{1,0:T(8,128)(2,1)} custom-call(bf16[1280,1024]{1,0:T(8,128)(2,1)} %get-tuple-element.10.hid_ref, bf16[512,1280]{1,0:T(8,128)(2,1)} %get-tuple-element.11.mix_hbm_g, bf16[512,1280]{1,0:T(8,128)(2,1)} %get-tuple-element.12.mix_hbm_x, bf16[512,1280]{1,0:T(8,128)(2,1)} %get-tuple-element.13.mix_hbm_z, ...), custom_call_target="tpu_custom_call" | custom-call | tf_op jit(solution)/shard_map/giveback/pallas_call | solution.py:757
  199.9 2.2 %copy.9 = bf16[128,3584]{1,0:T(8,128)(2,1)} copy(bf16[128,3584]{1,0:T(8,128)(2,1)} %giveback.1) | data formatting | bytes 1835008
